TPU v7x, 512 devices: a whole 4x4x16 slice. The times are simulated.
512 devices in a mesh: sec: 32 (over z, core), blk: 16 (over y, x).
Axes of the slice: x: 4, y: 4, z: 16, core: 2. Of those that a mesh axis runs over, the one named last changes fastest.
Arguments:
- left_env: bfloat16 [32, 14, 16, 256, 256], P('sec', None, 'blk'), may hold values from -0.375 to 0.375
- right_out: bfloat16 [32, 14, 16, 256, 256], P('sec', None, 'blk'), may hold values from -0.09375 to 0.09375
- onsite: bfloat16 [32, 16, 256, 256], P('sec', 'blk'), may hold values from -1 to 1
- start_state: float32 [32, 16, 256, 256], P('sec', 'blk'), may hold values from -40 to 40
- live: int32 [32, 16], P('sec', 'blk'), may hold values from 64 to 256, as said below
- rank: int32 [32, 16], P('sec', 'blk'), may hold values from 1 to 256, as said below
- shift: int32 [14], replicated, may hold values from -1 to 1
Outputs:
- theta_out: float32 [32, 16, 256, 256], P('sec', 'blk')
- energies: float32 [32], P('sec')
- density: float32 [32, 16, 256, 256], P('sec', 'blk')
Inputs may be any that keep to these rules, and one draw needn't show every extreme that they name: live rows of a padded block; the middle block 8 of every section is full. Kept rank of a block, never more than its live rows; the middle block of every section keeps all 256.
All inputs are finite; a program needn't handle non-finite values.
Results may differ from a plain program's by a relative error of at most 0.003.
Values may be sent and summed in bfloat16 or wider, within the bound.
No kernel may reach another device: no remote copies, remote signals or barrier semaphores. Data moves between devices by JAX's collectives and lax.ppermute only.
A program may use at most 64 MiB of HBM per device.

v0:
```python
import jax
import jax.numpy as jnp
from jax import lax
from jax.sharding import PartitionSpec as P

ITERS = 3


def from_behind(block, axis, distance):
    devices = range(lax.axis_size(axis))
    route = [(i - distance, i) for i in devices if i - distance in devices]
    return lax.ppermute(block, axis, route)


def padded(array, sides, width):
    for axis, dim in sides:
        count, length = (lax.axis_size(axis), array.shape[dim])
        up = [(i, (i + 1) % count) for i in range(count - 1)]
        down = [(j, i) for i, j in up]
        last = lax.slice_in_dim(array, length - width, length, axis=dim)
        leading = lax.slice_in_dim(array, 0, width, axis=dim)
        before = lax.ppermute(last, axis, up)
        after = lax.ppermute(leading, axis, down)
        array = jnp.concatenate([before, array, after], axis=dim)
    return array


def per_device(left_env, right_out, onsite, start_state, live, rank, shift):
    left_blocks = left_env[0]
    onsite_blocks = onsite[0]
    right_env = from_behind(right_out[0], "sec", -1)
    state = start_state[0]
    block_count = state.shape[0]
    width = state.shape[1]
    positions = jnp.arange(width, dtype=jnp.int32)
    inside = positions[None, :] < live[0][:, None]
    cell_mask = (inside[:, :, None] & inside[:, None, :]).astype(jnp.float32)
    state = state * cell_mask
    offsets = jnp.arange(block_count, dtype=jnp.int32)[None, :] + shift[:, None]
    rim_partner = offsets + block_count
    energy = jnp.zeros((), jnp.float32)
    for iteration in range(ITERS):
        state_half = state.astype(jnp.bfloat16)
        source = padded(state_half, (("blk", 0),), block_count)
        picked = jnp.take(source, rim_partner, axis=0)
        inner = jnp.einsum(
            "kbij,kbjl->kbil", left_blocks, picked, preferred_element_type=jnp.float32
        ).astype(jnp.bfloat16)
        applied = jnp.einsum("kbil,kbml->bim", inner, right_env, preferred_element_type=jnp.float32)
        applied = applied + jnp.einsum(
            "bij,bjl->bil", onsite_blocks, state_half, preferred_element_type=jnp.float32
        )
        applied = applied + jnp.einsum(
            "bil,bml->bim", state_half, onsite_blocks, preferred_element_type=jnp.float32
        )
        applied = applied * cell_mask
        correlation, weight = lax.psum((jnp.sum(state * applied), jnp.sum(state * state)), "blk")
        energy = correlation / weight
        resid = applied - energy * state
        resid_norm = lax.psum(jnp.sum(resid * resid), "blk")
        state = (state - 0.3 * resid) / jnp.sqrt(1.0 + 0.09 * resid_norm / weight)
    final_half = state.astype(jnp.bfloat16)
    beside = from_behind(final_half, "sec", -1)
    keep = (positions[None, :] < rank[0][:, None]).astype(jnp.bfloat16)
    own_part = jnp.einsum(
        "bij,bmj->bim",
        final_half * keep[:, None, :],
        final_half,
        preferred_element_type=jnp.float32,
    )
    other_part = jnp.einsum(
        "bji,bjm->bim", beside * keep[:, :, None], beside, preferred_element_type=jnp.float32
    )
    return (state[None], energy.reshape(1), (own_part + other_part)[None])


def solution(mesh):
    placed = (
        P("sec", None, "blk", None, None),
        P("sec", None, "blk", None, None),
        P("sec", "blk", None, None),
        P("sec", "blk", None, None),
        P("sec", "blk"),
        P("sec", "blk"),
        P(),
    )
    return jax.shard_map(
        per_device,
        mesh=mesh,
        in_specs=placed,
        out_specs=(P("sec", "blk", None, None), P("sec"), P("sec", "blk", None, None)),
        check_vma=False,
    )
```

profile of v0, /device:TPU:97, one launch (start us, length us, event | category | flops | bytes accessed | tf_op | source)
XLA Modules:
  0.0 306.2 jit_solution(4411914146119246037)
XLA Ops:
  0.7 2.7 collective-permute-start.2
  5.1 3.1 %collective-permute-start = (bf16[1,256,256]{2,1,0:T(8,128)(2,1)S(1)}, bf16[1,256,256]{2,1,0:T(8,128)(2,1)S(1)}, u32[]{:S(2)}, u32[]{:S(2)}) collective-permute-start(bf16[1,256,256]{2,1,0:T(8,128)(2,1)S(1)} %fusion.163), channel_id=1, source_target_pairs={{0,1},{1,2},{2,3},{3,4},{4,5},{5,6},{6,7},{7,8},{8,9},{9,10},{10,1... | collective-permute-start | bytes 393224 | tf_op jit(solution)/shard_map/ppermute | solution.py:22
  8.2 1.3 collective-permute-start.1
  14.9 1.9 gather_fusion
  16.9 10.5 %collective-permute-done.2 = bf16[14,1,256,256]{3,2,0,1:T(8,128)(2,1)} collective-permute-done((bf16[14,1,256,256]{3,2,0,1:T(8,128)(2,1)}, bf16[14,1,256,256]{3,2,0,1:T(8,128)(2,1)}, u32[]{:S(2)}, u32[]{:S(2)}) %collective-permute-start.2) | collective-permute-done | bytes 1835040 | tf_op jit(solution)/shard_map/ppermute | solution.py:12
  27.3 4.0 %multiply_reduce_fusion.8 = (f32[]{:T(128)}, f32[256,256]{1,0:T(8,128)S(1)}) fusion(f32[1,1,256,256]{3,2,1,0:T(8,128)S(1)} %copy-done.1, pred[256]{0:T(512)(128)(4,1)S(1)} %iota_compare_fusion, f32[256,256]{1,0:T(8,128)S(1)} %fusion.175, f32[256,256]{1,0:T(8,128)S(1)} %convolution_bitcast_fusion.2, bf16[14,1,256,256]{3,2,0,1:T(8,128)(2,1)} %collective-permute-done.2, ...), kind=kOutput, calls=%fused_computation.69 | convolution fusion | flops 941817856 | bytes 6553874 | tf_op jit(solution)/shard_map/kbil,kbml->bim/dot_general | solution.py:49
  31.3 34.5 %all-reduce.2 = (f32[]{:T(128)}, f32[]{:T(128)}) all-reduce(f32[]{:T(128)} %get-tuple-element.20, f32[]{:T(128)} %multiply_reduce_fusion.7), channel_id=1, replica_groups=mesh['sec'=32,'blk'=16] {'blk'}, use_global_device_ids=true, to_apply=%region_1.3 | all-reduce | flops 2 | bytes 16 | tf_op jit(solution)/shard_map/psum | solution.py:57
  67.9 29.4 %psum.65 = f32[]{:T(128)} all-reduce(f32[]{:T(128)} %multiply_reduce_fusion.6), channel_id=1, replica_groups=mesh['sec'=32,'blk'=16] {'blk'}, use_global_device_ids=true, to_apply=%region_5.7 | all-reduce | flops 1 | bytes 8 | tf_op jit(solution)/shard_map/psum | solution.py:60
  98.9 3.5 %collective-permute-start.3 = (bf16[1,256,256]{2,1,0:T(8,128)(2,1)S(1)}, bf16[1,256,256]{2,1,0:T(8,128)(2,1)S(1)}, u32[]{:S(2)}, u32[]{:S(2)}) collective-permute-start(bf16[1,256,256]{2,1,0:T(8,128)(2,1)S(1)} %get-tuple-element.18), channel_id=1, source_target_pairs={{0,1},{1,2},{2,3},{3,4},{4,5},{5,6},{6,7},{7,8},{8,9},{9,10},{10,1... | collective-permute-start | bytes 393224 | tf_op jit(solution)/shard_map/ppermute | solution.py:22
  102.4 1.3 collective-permute-start.4
  104.3 3.8 %collective-permute-done.4 = bf16[1,256,256]{2,1,0:T(8,128)(2,1)S(1)} collective-permute-done((bf16[1,256,256]{2,1,0:T(8,128)(2,1)S(1)}, bf16[1,256,256]{2,1,0:T(8,128)(2,1)S(1)}, u32[]{:S(2)}, u32[]{:S(2)}) %collective-permute-start.4) | collective-permute-done | bytes 131104 | tf_op jit(solution)/shard_map/ppermute | solution.py:23
  108.2 1.9 gather_fusion.1
  110.1 4.0 %multiply_reduce_fusion.4 = (f32[]{:T(128)}, f32[]{:T(128)}, f32[256,256]{1,0:T(8,128)S(1)}) fusion(f32[256,256]{1,0:T(8,128)S(1)} %get-tuple-element.19, f32[256,256]{1,0:T(8,128)S(1)} %fusion.172, f32[256,256]{1,0:T(8,128)S(1)} %convolution_bitcast_fusion.1, bf16[14,1,256,256]{3,2,0,1:T(8,128)(2,1)} %collective-permute-done.2, ...), kind=kOutput, calls=%fused_computation.63 | convolution fusion | flops 941883392 | bytes 6553878 | tf_op jit(solution)/shard_map/kbil,kbml->bim/dot_general | solution.py:49
  114.1 29.2 %all-reduce.1 = (f32[]{:T(128)}, f32[]{:T(128)}) all-reduce(f32[]{:T(128)} %get-tuple-element.7, f32[]{:T(128)} %get-tuple-element.6), channel_id=1, replica_groups=mesh['sec'=32,'blk'=16] {'blk'}, use_global_device_ids=true, to_apply=%region_7.9 | all-reduce | flops 2 | bytes 16 | tf_op jit(solution)/shard_map/psum | solution.py:57
  145.9 30.7 %psum.68 = f32[]{:T(128)} all-reduce(f32[]{:T(128)} %multiply_reduce_fusion.3), channel_id=1, replica_groups=mesh['sec'=32,'blk'=16] {'blk'}, use_global_device_ids=true, to_apply=%region_11.13 | all-reduce | flops 1 | bytes 8 | tf_op jit(solution)/shard_map/psum | solution.py:60
  178.1 2.1 collective-permute-start.5
  180.1 1.3 collective-permute-start.6
  182.1 3.8 %collective-permute-done.6 = bf16[1,256,256]{2,1,0:T(8,128)(2,1)S(1)} collective-permute-done((bf16[1,256,256]{2,1,0:T(8,128)(2,1)S(1)}, bf16[1,256,256]{2,1,0:T(8,128)(2,1)S(1)}, u32[]{:S(2)}, u32[]{:S(2)}) %collective-permute-start.6) | collective-permute-done | bytes 131104 | tf_op jit(solution)/shard_map/ppermute | solution.py:23
  185.9 1.9 gather_fusion.2
  187.8 4.0 %multiply_reduce_fusion.1 = (f32[]{:T(128)}, f32[]{:T(128)}, f32[256,256]{1,0:T(8,128)S(1)}) fusion(f32[256,256]{1,0:T(8,128)S(1)} %get-tuple-element.17, f32[256,256]{1,0:T(8,128)S(1)} %fusion.169, f32[256,256]{1,0:T(8,128)S(1)} %convolution_bitcast_fusion, bf16[14,1,256,256]{3,2,0,1:T(8,128)(2,1)} %collective-permute-done.2, ...), kind=kOutput, calls=%fused_computation.58 | convolution fusion | flops 941883392 | bytes 6553878 | tf_op jit(solution)/shard_map/kbil,kbml->bim/dot_general | solution.py:49
  191.8 29.2 %all-reduce = (f32[]{:T(128)}, f32[]{:T(128)}) all-reduce(f32[]{:T(128)} %get-tuple-element.5, f32[]{:T(128)} %get-tuple-element.4), channel_id=1, replica_groups=mesh['sec'=32,'blk'=16] {'blk'}, use_global_device_ids=true, to_apply=%region_13.15 | all-reduce | flops 2 | bytes 16 | tf_op jit(solution)/shard_map/psum | solution.py:57
  223.0 30.5 %psum.71 = f32[]{:T(128)} all-reduce(f32[]{:T(128)} %multiply_reduce_fusion), channel_id=1, replica_groups=mesh['sec'=32,'blk'=16] {'blk'}, use_global_device_ids=true, to_apply=%region_17.19 | all-reduce | flops 1 | bytes 8 | tf_op jit(solution)/shard_map/psum | solution.py:60
  254.9 43.8 %collective-permute-start.7 = (bf16[1,256,256]{2,1,0:T(8,128)(2,1)S(1)}, bf16[1,256,256]{2,1,0:T(8,128)(2,1)S(1)}, u32[]{:S(2)}, u32[]{:S(2)}) collective-permute-start(bf16[1,256,256]{2,1,0:T(8,128)(2,1)S(1)} %get-tuple-element.14), channel_id=1, source_target_pairs={{16,0},{32,16},{48,32},{64,48},{80,64},{96,80},{112,96},{128,112},... | collective-permute-start | bytes 393224 | tf_op jit(solution)/shard_map/ppermute | solution.py:12
  299.0 5.1 %collective-permute-done.7 = bf16[1,256,256]{2,1,0:T(8,128)(2,1)S(1)} collective-permute-done((bf16[1,256,256]{2,1,0:T(8,128)(2,1)S(1)}, bf16[1,256,256]{2,1,0:T(8,128)(2,1)S(1)}, u32[]{:S(2)}, u32[]{:S(2)}) %collective-permute-start.7) | collective-permute-done | bytes 131104 | tf_op jit(solution)/shard_map/ppermute | solution.py:12
  (36 shorter events, 11.3 us)
Async XLA Ops:
  0.6 26.7 %copy-start = (bf16[1,14,1,256,256]{4,3,2,1,0:T(8,128)(2,1)S(1)}, bf16[1,14,1,256,256]{4,3,2,1,0:T(8,128)(2,1)}, u32[]{:S(2)}) copy-start(bf16[1,14,1,256,256]{4,3,2,1,0:T(8,128)(2,1)} %param.9) | copy-start | bytes 5505028
  0.6 12.7 %copy-start.1 = (f32[1,1,256,256]{3,2,1,0:T(8,128)S(1)}, f32[1,1,256,256]{3,2,1,0:T(8,128)}, u32[]{:S(2)}) copy-start(f32[1,1,256,256]{3,2,1,0:T(8,128)} %param.12) | copy-start | bytes 786436
  0.7 26.7 %collective-permute-start.2 = (bf16[14,1,256,256]{3,2,0,1:T(8,128)(2,1)}, bf16[14,1,256,256]{3,2,0,1:T(8,128)(2,1)}, u32[]{:S(2)}, u32[]{:S(2)}) collective-permute-start(bf16[14,1,256,256]{3,2,0,1:T(8,128)(2,1)} %bitcast.331), channel_id=1, source_target_pairs={{16,0},{32,16},{48,32},{64,48},{80,64},{96,80},{112,96},{128,112},... | collective-permute-start | bytes 5505032 | tf_op jit(solution)/shard_map/ppermute | solution.py:12
  5.1 9.0 %collective-permute-start = (bf16[1,256,256]{2,1,0:T(8,128)(2,1)S(1)}, bf16[1,256,256]{2,1,0:T(8,128)(2,1)S(1)}, u32[]{:S(2)}, u32[]{:S(2)}) collective-permute-start(bf16[1,256,256]{2,1,0:T(8,128)(2,1)S(1)} %fusion.163), channel_id=1, source_target_pairs={{0,1},{1,2},{2,3},{3,4},{4,5},{5,6},{6,7},{7,8},{8,9},{9,10},{10,1... | collective-permute-start | bytes 393224 | tf_op jit(solution)/shard_map/ppermute | solution.py:22
  8.2 6.7 %collective-permute-start.1 = (bf16[1,256,256]{2,1,0:T(8,128)(2,1)S(1)}, bf16[1,256,256]{2,1,0:T(8,128)(2,1)S(1)}, u32[]{:S(2)}, u32[]{:S(2)}) collective-permute-start(bf16[1,256,256]{2,1,0:T(8,128)(2,1)S(1)} %fusion.163), channel_id=1, source_target_pairs={{1,0},{2,1},{3,2},{4,3},{5,4},{6,5},{7,6},{8,7},{9,8},{10,9},{11,1... | collective-permute-start | bytes 393224 | tf_op jit(solution)/shard_map/ppermute | solution.py:23
  16.9 86.9 %copy-start.2 = (bf16[1,1,256,256]{3,2,1,0:T(8,128)(2,1)S(1)}, bf16[1,1,256,256]{3,2,1,0:T(8,128)(2,1)}, u32[]{:S(2)}) copy-start(bf16[1,1,256,256]{3,2,1,0:T(8,128)(2,1)} %param.11) | copy-start | bytes 393220
  98.9 5.5 %collective-permute-start.3 = (bf16[1,256,256]{2,1,0:T(8,128)(2,1)S(1)}, bf16[1,256,256]{2,1,0:T(8,128)(2,1)S(1)}, u32[]{:S(2)}, u32[]{:S(2)}) collective-permute-start(bf16[1,256,256]{2,1,0:T(8,128)(2,1)S(1)} %get-tuple-element.18), channel_id=1, source_target_pairs={{0,1},{1,2},{2,3},{3,4},{4,5},{5,6},{6,7},{7,8},{8,9},{9,10},{10,1... | collective-permute-start | bytes 393224 | tf_op jit(solution)/shard_map/ppermute | solution.py:22
  102.4 5.7 %collective-permute-start.4 = (bf16[1,256,256]{2,1,0:T(8,128)(2,1)S(1)}, bf16[1,256,256]{2,1,0:T(8,128)(2,1)S(1)}, u32[]{:S(2)}, u32[]{:S(2)}) collective-permute-start(bf16[1,256,256]{2,1,0:T(8,128)(2,1)S(1)} %get-tuple-element.18), channel_id=1, source_target_pairs={{1,0},{2,1},{3,2},{4,3},{5,4},{6,5},{7,6},{8,7},{9,8},{10,9},{11,1... | collective-permute-start | bytes 393224 | tf_op jit(solution)/shard_map/ppermute | solution.py:23
  178.1 4.0 %collective-permute-start.5 = (bf16[1,256,256]{2,1,0:T(8,128)(2,1)S(1)}, bf16[1,256,256]{2,1,0:T(8,128)(2,1)S(1)}, u32[]{:S(2)}, u32[]{:S(2)}) collective-permute-start(bf16[1,256,256]{2,1,0:T(8,128)(2,1)S(1)} %get-tuple-element.16), channel_id=1, source_target_pairs={{0,1},{1,2},{2,3},{3,4},{4,5},{5,6},{6,7},{7,8},{8,9},{9,10},{10,1... | collective-permute-start | bytes 393224 | tf_op jit(solution)/shard_map/ppermute | solution.py:22
  180.1 5.7 %collective-permute-start.6 = (bf16[1,256,256]{2,1,0:T(8,128)(2,1)S(1)}, bf16[1,256,256]{2,1,0:T(8,128)(2,1)S(1)}, u32[]{:S(2)}, u32[]{:S(2)}) collective-permute-start(bf16[1,256,256]{2,1,0:T(8,128)(2,1)S(1)} %get-tuple-element.16), channel_id=1, source_target_pairs={{1,0},{2,1},{3,2},{4,3},{5,4},{6,5},{7,6},{8,7},{9,8},{10,9},{11,1... | collective-permute-start | bytes 393224 | tf_op jit(solution)/shard_map/ppermute | solution.py:23
  254.9 50.2 %copy-start.3 = (f32[256,256]{1,0:T(8,128)}, f32[256,256]{1,0:T(8,128)S(1)}, u32[]{:S(2)}) copy-start(f32[256,256]{1,0:T(8,128)S(1)} %get-tuple-element.15) | copy-start | bytes 786436
  254.9 49.1 %collective-permute-start.7 = (bf16[1,256,256]{2,1,0:T(8,128)(2,1)S(1)}, bf16[1,256,256]{2,1,0:T(8,128)(2,1)S(1)}, u32[]{:S(2)}, u32[]{:S(2)}) collective-permute-start(bf16[1,256,256]{2,1,0:T(8,128)(2,1)S(1)} %get-tuple-element.14), channel_id=1, source_target_pairs={{16,0},{32,16},{48,32},{64,48},{80,64},{96,80},{112,96},{128,112},... | collective-permute-start | bytes 393224 | tf_op jit(solution)/shard_map/ppermute | solution.py:12
where the time goes:
time: 307 us; the launch traced here: 306 us
  blocking collectives  184 us (60%)
  starting transfers between devices  59.1 us (19%)
  waiting for transfers between devices  24.3 us (8%)
  matrix products  16.4 us (5%)
  between operations  11.4 us (4%)
  local copies, waits for them, and re-layouts  5.78 us (2%)
  other arithmetic  5.62 us (2%)
    psum x3, blocking collectives, per_device(): lax.psum((jnp.sum(state * applied), jnp.sum(state * state)), 'blk')  92.8 us
    psum x3, blocking collectives, per_device(): resid_norm = lax.psum(jnp.sum(resid * resid), 'blk')  90.7 us
    ppermute x2, starting transfers between devices, from_behind(): return lax.ppermute(block, axis, route)  46.5 us
    ppermute x2, waiting for transfers between devices, from_behind(): return lax.ppermute(block, axis, route)  15.6 us
    dot_general x3, matrix products, per_device(): jnp.einsum('kbil,kbml->bim', inner, right_env, preferred_element_type=jnp...  11.9 us
    ppermute x3, starting transfers between devices, padded(): before = lax.ppermute(last, axis, up)  8.72 us
    ppermute x3, waiting for transfers between devices, padded(): after = lax.ppermute(leading, axis, down)  8.34 us
  transfers between devices with their start and end apart: 8, of which 7 were waited for; matrix products, arithmetic and copies ran while one was open for 3% of the time, Pallas kernels for 0%

commit v1 on v0

v1 whole, which is shorter than its diff:
```python
import functools

import jax
import jax.numpy as jnp
from jax import lax
from jax.experimental import pallas as pl
from jax.experimental.pallas import tpu as pltpu
from jax.sharding import PartitionSpec as P

STEP = 0.3
VM = pl.BlockSpec(memory_space=pltpu.VMEM)
SM = pl.BlockSpec(memory_space=pltpu.SMEM)
F32 = jnp.float32
BF = jnp.bfloat16
LIMIT = 20 * 1024 * 1024


def call(body, outs, args, specs, scratch=(), flops=10**8, out_specs=None):
    moved = sum(a.size * a.dtype.itemsize for a in args)
    return pl.pallas_call(
        body,
        out_shape=[jax.ShapeDtypeStruct(s, d) for s, d in outs],
        in_specs=specs,
        out_specs=out_specs or [VM] * len(outs),
        scratch_shapes=list(scratch),
        compiler_params=pltpu.CompilerParams(vmem_limit_bytes=LIMIT),
        cost_estimate=pl.CostEstimate(flops=flops, bytes_accessed=moved, transcendentals=0),
    )(*args)


def dot(a, b):
    return jnp.dot(a, b, preferred_element_type=F32)


def dot_t(a, b):
    return lax.dot_general(a, b, (((1,), (1,)), ((), ())), preferred_element_type=F32)


def inside(live, shape):
    rows = lax.broadcasted_iota(jnp.int32, shape, 0)
    cols = lax.broadcasted_iota(jnp.int32, shape, 1)
    return (rows < live) & (cols < live)


def init_body(live, start, p_ref, h_ref):
    p = jnp.where(inside(live[0, 0], start.shape), start[...], 0.0)
    p_ref[...] = p
    h_ref[...] = p.astype(BF)


def fill(hs, before, own, after):
    hs[0] = before[...]
    hs[1] = own[...]
    hs[2] = after[...]


def inner_body(shift, left, before, own, after, onsite, inner, total, hs):
    fill(hs, before, own, after)
    h = own[...]
    total[...] = dot(onsite[...], h) + dot_t(h, onsite[...])
    for k in range(left.shape[0]):
        inner[k] = dot(left[k], hs[shift[k] + 1]).astype(BF)


def finish(total, live, p, w_ref, p_ref, h_ref):
    w = jnp.where(inside(live, total.shape), total, 0.0)
    w_ref[...] = w
    q = p - STEP * w
    p_ref[...] = q
    h_ref[...] = q.astype(BF)
    return w, q


def outer_body(live, inner, right, start, p, w_ref, p_ref, h_ref):
    total = start[...]
    for k in range(right.shape[0]):
        total = total + dot_t(inner[k], right[k])
    finish(total, live[0, 0], p[...], w_ref, p_ref, h_ref)


def both_body(shift, live, left, right, before, own, after, onsite, p, w_ref, p_ref, h_ref, hs):
    fill(hs, before, own, after)
    h = own[...]
    total = dot(onsite[...], h) + dot_t(h, onsite[...])
    for k in range(left.shape[0]):
        part = dot(left[k], hs[shift[k] + 1]).astype(BF)
        total = total + dot_t(part, right[k])
    finish(total, live[0, 0], p[...], w_ref, p_ref, h_ref)


def gram_body(p0, w0, w1, w2, g_ref):
    a, b, c, d = p0[...], w0[...], w1[...], w2[...]
    pairs = ((a, a), (a, b), (a, c), (a, d), (b, b), (b, c), (b, d), (c, c), (c, d), (d, d))
    lane = lax.broadcasted_iota(jnp.int32, g_ref.shape, 1)
    out = jnp.zeros(g_ref.shape, F32)
    for i, (x, y) in enumerate(pairs):
        out = jnp.where(lane == i, jnp.sum(x * y), out)
    g_ref[...] = out


def final_body(parts, p0, p1, p2, p3, theta_ref, half_ref, energy_ref):
    sums = jnp.sum(parts[...], axis=0, keepdims=True)
    v = [sums[:, i : i + 1] for i in range(10)]
    weight, p0w = v[0], [v[1], v[2], v[3]]
    ww = [[v[4], v[5], v[6]], [v[5], v[7], v[8]], [v[6], v[8], v[9]]]
    p1w = [p0w[j] - STEP * ww[0][j] for j in range(3)]
    p2w = [p1w[j] - STEP * ww[1][j] for j in range(3)]
    pw = [p0w, p1w, p2w]
    one = jnp.ones_like(weight)
    coef, scale = [one], one
    energy = one
    for n in range(3):
        c = jnp.zeros_like(one)
        a = jnp.zeros_like(one)
        for i in range(n + 1):
            for j in range(n + 1):
                t = coef[i] * coef[j]
                c = c + t * pw[i][j]
                a = a + t * ww[i][j]
        energy = c * scale / weight
        excess = jnp.maximum(a * scale / weight - energy * energy, 0.0)
        scale = scale / (1.0 + STEP * STEP * excess)
        g = STEP * energy
        coef = [g * coef[0]] + [coef[i - 1] + g * coef[i] for i in range(1, n + 1)] + [one]
    energy_ref[...] = jnp.broadcast_to(energy, energy_ref.shape)
    root = jnp.sqrt(scale)
    theta = (root * coef[0]) * p0[...] + (root * coef[1]) * p1[...]
    theta = theta + (root * coef[2]) * p2[...] + root * p3[...]
    theta_ref[...] = theta
    half_ref[...] = theta.astype(BF)


def per_device(left_env, right_out, onsite, start_state, live, rank, shift):
    terms, width = left_env.shape[1], left_env.shape[-1]
    square = (width, width)
    left = left_env.reshape(terms, *square)
    onsite = onsite.reshape(square)
    sections, blocks = lax.axis_size("sec"), lax.axis_size("blk")
    ahead = [(i + 1, i) for i in range(sections - 1)]
    up = [(i, i + 1) for i in range(blocks - 1)]
    down = [(i + 1, i) for i in range(blocks - 1)]
    right = lax.ppermute(right_out.reshape(terms, *square), "sec", ahead)
    state = start_state.reshape(square)
    p0, h0 = call(init_body, [(square, F32), (square, BF)], (live, state), [SM, VM])

    def halo(h):
        return lax.ppermute(h, "blk", up), h, lax.ppermute(h, "blk", down)

    triple = [(square, F32), (square, F32), (square, BF)]
    slots = [pltpu.VMEM((3, *square), BF)]
    inner, total = call(
        inner_body,
        [((terms, *square), BF), (square, F32)],
        (shift, left, *halo(h0), onsite),
        [SM] + [VM] * 5,
        slots,
    )
    w0, p1, h1 = call(outer_body, triple, (live, inner, right, total, p0), [SM] + [VM] * 4)

    def both(h, p):
        args = (shift, live, left, right, *halo(h), onsite, p)
        return call(both_body, triple, args, [SM, SM] + [VM] * 7, slots)

    w1, p2, h2 = both(h1, p1)
    w2, p3, _ = both(h2, p2)
    (gram,) = call(gram_body, [((blocks, 128), F32)], (p0, w0, w1, w2), [VM] * 4)
    parts = lax.all_to_all(gram, "blk", 0, 0, tiled=True)
    theta, half, energy = call(
        final_body, [(square, F32), (square, BF), ((1, 128), F32)], (parts, p0, p1, p2, p3), [VM] * 5
    )
    beside = lax.ppermute(half, "sec", ahead)
    keep = (jnp.arange(width, dtype=jnp.int32) < rank[0, 0]).astype(BF)
    own_part = dot_t(half * keep[None, :], half)
    other_part = lax.dot_general(
        beside * keep[:, None], beside, (((0,), (0,)), ((), ())), preferred_element_type=F32
    )
    density = own_part + other_part
    return theta[None, None], energy[0, :1], density[None, None]


def solution(mesh):
    placed = (
        P("sec", None, "blk", None, None),
        P("sec", None, "blk", None, None),
        P("sec", "blk", None, None),
        P("sec", "blk", None, None),
        P("sec", "blk"),
        P("sec", "blk"),
        P(),
    )
    return jax.shard_map(
        per_device,
        mesh=mesh,
        in_specs=placed,
        out_specs=(P("sec", "blk", None, None), P("sec"), P("sec", "blk", None, None)),
        check_vma=False,
    )
```

time: 307 us -> 79 us (0.26)
  blocking collectives: 184 us -> 15.2 us
  starting transfers between devices: 59.1 us -> 18.9 us
  matrix products: 16.4 us -> 1.24 us
  between operations: 11.4 us -> 2.05 us
  Pallas kernels: 0 us -> 8.23 us
  other arithmetic: 5.62 us -> 0.01 us
  waiting for transfers between devices: 24.3 us -> 28.9 us
    psum x6 -> x0, blocking collectives: 184 us -> none  [the longest x3 92.8 us: per_device(): lax.psum((jnp.sum(state * applied), jnp.sum(state * state)), 'blk')]
    ppermute x8, starting transfers between devices: 59.1 us -> 18.9 us  [the longest x6 13.2 us: halo(): return (lax.ppermute(h, 'blk', up), h, lax.ppermute(h, 'blk', down))]
    dot_general x11 -> x2, matrix products: 16.4 us -> 1.24 us  [the longest x1 0.93 us: dot_t(): lax.dot_general(a, b, (((1,), (1,)), ((), ())), preferred_element_type=F32)]
    all_to_all x0 -> x1, blocking collectives: none -> 15.2 us  [per_device(): parts = lax.all_to_all(gram, 'blk', 0, 0, tiled=True)]
    pallas_call x0 -> x7, Pallas kernels: none -> 8.23 us  [call(): pl.pallas_call(body, out_shape=[jax.ShapeDtypeStruct(s, d) for s, d in ou...]
    gather x3 -> x0, local copies, waits for them, and re-layouts: 5.76 us -> none  [per_device(): picked = jnp.take(source, rim_partner, axis=0)]
    ppermute x8, waiting for transfers between devices: 24.3 us -> 28.9 us  [the longest x6 15 us: halo(): return (lax.ppermute(h, 'blk', up), h, lax.ppermute(h, 'blk', down))]
    unnamed x8 -> x14, local copies, waits for them, and re-layouts: 0.03 us -> 4.01 us
  transfers between devices with their start and end apart: 8 -> 8, of which waited for: 7 -> 8; matrix products, arithmetic and copies ran while one was open for 3% -> 0% of each run, Pallas kernels for 0% -> 2%
where the time goes in v1:
time: 79 us; the launch traced here: 78.5 us
  waiting for transfers between devices  28.9 us (37%)
  starting transfers between devices  18.9 us (24%)
  blocking collectives  15.2 us (19%)
  Pallas kernels  8.23 us (10%)
  local copies, waits for them, and re-layouts  4.01 us (5%)
  between operations  2.05 us (3%)
  matrix products  1.24 us (2%)
    all_to_all x1, blocking collectives, per_device(): parts = lax.all_to_all(gram, 'blk', 0, 0, tiled=True)  15.2 us
    ppermute x6, waiting for transfers between devices, halo(): return (lax.ppermute(h, 'blk', up), h, lax.ppermute(h, 'blk', down))  15 us
    ppermute x6, starting transfers between devices, halo(): return (lax.ppermute(h, 'blk', up), h, lax.ppermute(h, 'blk', down))  13.2 us
    pallas_call x7, Pallas kernels, call(): pl.pallas_call(body, out_shape=[jax.ShapeDtypeStruct(s, d) for s, d in ou...  8.23 us
    ppermute x1, waiting for transfers between devices, per_device(): right = lax.ppermute(right_out.reshape(terms, *square), 'sec', ahead)  8.06 us
    ppermute x1, waiting for transfers between devices, per_device(): beside = lax.ppermute(half, 'sec', ahead)  5.88 us
    unnamed x14, local copies, waits for them, and re-layouts  4.01 us
    ppermute x1, starting transfers between devices, per_device(): beside = lax.ppermute(half, 'sec', ahead)  3.11 us
  transfers between devices with their start and end apart: 8, of which 8 were waited for; matrix products, arithmetic and copies ran while one was open for 0% of the time, Pallas kernels for 2%

profile of v1, /device:TPU:97, one launch (start us, length us, event | category | flops | bytes accessed | tf_op | source)
XLA Modules:
  0.0 78.5 jit_solution(17598135194037987590)
XLA Ops:
  0.6 2.6 %collective-permute-start.2 = (bf16[14,256,256]{2,1,0:T(8,128)(2,1)}, bf16[14,256,256]{2,1,0:T(8,128)(2,1)S(1)}, u32[]{:S(2)}, u32[]{:S(2)}) collective-permute-start(bf16[14,256,256]{2,1,0:T(8,128)(2,1)} %bitcast.26), channel_id=1, source_target_pairs={{16,0},{32,16},{48,32},{64,48},{80,64},{96,80},{112,96},{128,112},... | collective-permute-start | bytes 5505032 | tf_op jit(solution)/shard_map/ppermute | solution.py:142
  3.9 0.9 %copy-done.6 = f32[1,1,256,256]{3,2,1,0:T(8,128)S(1)} copy-done((f32[1,1,256,256]{3,2,1,0:T(8,128)S(1)}, f32[1,1,256,256]{3,2,1,0:T(8,128)}, u32[]{:S(2)}) %copy-start.6) | copy-done | bytes 262168
  4.9 3.1 %collective-permute-start = (bf16[256,256]{1,0:T(8,128)(2,1)S(1)}, bf16[256,256]{1,0:T(8,128)(2,1)S(1)}, u32[]{:S(2)}, u32[]{:S(2)}) collective-permute-start(bf16[256,256]{1,0:T(8,128)(2,1)S(1)} %get-tuple-element.19.own), channel_id=1, source_target_pairs={{0,1},{1,2},{2,3},{3,4},{4,5},{5,6},{6,7},{7,8},{8,9},{9,10},{10,1... | collective-permute-start | bytes 393224 | tf_op jit(solution)/shard_map/ppermute | solution.py:147
  8.0 1.3 %collective-permute-start.1 = (bf16[256,256]{1,0:T(8,128)(2,1)S(1)}, bf16[256,256]{1,0:T(8,128)(2,1)S(1)}, u32[]{:S(2)}, u32[]{:S(2)}) collective-permute-start(bf16[256,256]{1,0:T(8,128)(2,1)S(1)} %get-tuple-element.19.own), channel_id=1, source_target_pairs={{1,0},{2,1},{3,2},{4,3},{5,4},{6,5},{7,6},{8,7},{9,8},{10,9},{11,1... | collective-permute-start | bytes 393224 | tf_op jit(solution)/shard_map/ppermute | solution.py:147
  9.3 1.5 %collective-permute-done.before = bf16[256,256]{1,0:T(8,128)(2,1)S(1)} collective-permute-done((bf16[256,256]{1,0:T(8,128)(2,1)S(1)}, bf16[256,256]{1,0:T(8,128)(2,1)S(1)}, u32[]{:S(2)}, u32[]{:S(2)}) %collective-permute-start) | collective-permute-done | bytes 131104 | tf_op jit(solution)/shard_map/ppermute | solution.py:147
  10.8 3.8 %collective-permute-done.1.after = bf16[256,256]{1,0:T(8,128)(2,1)S(1)} collective-permute-done((bf16[256,256]{1,0:T(8,128)(2,1)S(1)}, bf16[256,256]{1,0:T(8,128)(2,1)S(1)}, u32[]{:S(2)}, u32[]{:S(2)}) %collective-permute-start.1) | collective-permute-done | bytes 131104 | tf_op jit(solution)/shard_map/ppermute | solution.py:147
  14.6 1.5 %copy-done = bf16[1,14,1,256,256]{4,3,2,1,0:T(8,128)(2,1)S(1)} copy-done((bf16[1,14,1,256,256]{4,3,2,1,0:T(8,128)(2,1)S(1)}, bf16[1,14,1,256,256]{4,3,2,1,0:T(8,128)(2,1)}, u32[]{:S(2)}) %copy-start) | copy-done | bytes 1835032
  16.1 0.9 %copy-done.2 = bf16[1,1,256,256]{3,2,1,0:T(8,128)(2,1)S(1)} copy-done((bf16[1,1,256,256]{3,2,1,0:T(8,128)(2,1)S(1)}, bf16[1,1,256,256]{3,2,1,0:T(8,128)(2,1)}, u32[]{:S(2)}) %copy-start.2) | copy-done | bytes 131096
  17.7 1.3 %shard_map.95 = (bf16[14,256,256]{2,1,0:T(8,128)(2,1)S(1)}, f32[256,256]{1,0:T(8,128)S(1)}) custom-call(s32[14]{0:T(128)S(1)} %copy-done.4, bf16[14,256,256]{2,1,0:T(8,128)(2,1)S(1)} %bitcast.17, bf16[256,256]{1,0:T(8,128)(2,1)S(1)} %collective-permute-done.before, bf16[256,256]{1,0:T(8,128)(2,1)S(1)} %get-tuple-element.19.own, ...), custom_call_target="tpu_custom_call" | custom-call | flops 100000000 | bytes 2359352 | tf_op jit(solution)/shard_map/pallas_call | solution.py:20
  19.0 8.1 %collective-permute-done.2.right = bf16[14,256,256]{2,1,0:T(8,128)(2,1)S(1)} collective-permute-done((bf16[14,256,256]{2,1,0:T(8,128)(2,1)}, bf16[14,256,256]{2,1,0:T(8,128)(2,1)S(1)}, u32[]{:S(2)}, u32[]{:S(2)}) %collective-permute-start.2) | collective-permute-done | bytes 1835040 | tf_op jit(solution)/shard_map/ppermute | solution.py:142
  27.7 3.1 %collective-permute-start.3 = (bf16[256,256]{1,0:T(8,128)(2,1)S(1)}, bf16[256,256]{1,0:T(8,128)(2,1)S(1)}, u32[]{:S(2)}, u32[]{:S(2)}) collective-permute-start(bf16[256,256]{1,0:T(8,128)(2,1)S(1)} %get-tuple-element.23.own), channel_id=1, source_target_pairs={{0,1},{1,2},{2,3},{3,4},{4,5},{5,6},{6,7},{7,8},{8,9},{9,10},{10,1... | collective-permute-start | bytes 393224 | tf_op jit(solution)/shard_map/ppermute | solution.py:147
  30.9 1.3 %collective-permute-start.4 = (bf16[256,256]{1,0:T(8,128)(2,1)S(1)}, bf16[256,256]{1,0:T(8,128)(2,1)S(1)}, u32[]{:S(2)}, u32[]{:S(2)}) collective-permute-start(bf16[256,256]{1,0:T(8,128)(2,1)S(1)} %get-tuple-element.23.own), channel_id=1, source_target_pairs={{1,0},{2,1},{3,2},{4,3},{5,4},{6,5},{7,6},{8,7},{9,8},{10,9},{11,1... | collective-permute-start | bytes 393224 | tf_op jit(solution)/shard_map/ppermute | solution.py:147
  32.8 3.8 %collective-permute-done.4.after = bf16[256,256]{1,0:T(8,128)(2,1)S(1)} collective-permute-done((bf16[256,256]{1,0:T(8,128)(2,1)S(1)}, bf16[256,256]{1,0:T(8,128)(2,1)S(1)}, u32[]{:S(2)}, u32[]{:S(2)}) %collective-permute-start.4) | collective-permute-done | bytes 131104 | tf_op jit(solution)/shard_map/ppermute | solution.py:147
  36.6 1.9 %shard_map.97 = (f32[256,256]{1,0:T(8,128)S(1)}, f32[256,256]{1,0:T(8,128)S(1)}, bf16[256,256]{1,0:T(8,128)(2,1)S(1)}) custom-call(s32[14]{0:T(128)S(1)} %copy-done.5, s32[1,1]{1,0:T(1,128)S(6)} %copy.11.live, bf16[14,256,256]{2,1,0:T(8,128)(2,1)S(1)} %bitcast.18, bf16[14,256,256]{2,1,0:T(8,128)(2,1)S(1)} %collective-permute-done.2.right, ...), custom_call_target="tpu_custom_call" | custom-call | flops 100000000 | bytes 4456508 | tf_op jit(solution)/shard_map/pallas_call | solution.py:20
  38.5 3.1 %collective-permute-start.5 = (bf16[256,256]{1,0:T(8,128)(2,1)S(1)}, bf16[256,256]{1,0:T(8,128)(2,1)S(1)}, u32[]{:S(2)}, u32[]{:S(2)}) collective-permute-start(bf16[256,256]{1,0:T(8,128)(2,1)S(1)} %get-tuple-element.26.own), channel_id=1, source_target_pairs={{0,1},{1,2},{2,3},{3,4},{4,5},{5,6},{6,7},{7,8},{8,9},{9,10},{10,1... | collective-permute-start | bytes 393224 | tf_op jit(solution)/shard_map/ppermute | solution.py:147
  41.6 1.3 %collective-permute-start.6 = (bf16[256,256]{1,0:T(8,128)(2,1)S(1)}, bf16[256,256]{1,0:T(8,128)(2,1)S(1)}, u32[]{:S(2)}, u32[]{:S(2)}) collective-permute-start(bf16[256,256]{1,0:T(8,128)(2,1)S(1)} %get-tuple-element.26.own), channel_id=1, source_target_pairs={{1,0},{2,1},{3,2},{4,3},{5,4},{6,5},{7,6},{8,7},{9,8},{10,9},{11,1... | collective-permute-start | bytes 393224 | tf_op jit(solution)/shard_map/ppermute | solution.py:147
  42.9 1.1 %collective-permute-done.5.before = bf16[256,256]{1,0:T(8,128)(2,1)S(1)} collective-permute-done((bf16[256,256]{1,0:T(8,128)(2,1)S(1)}, bf16[256,256]{1,0:T(8,128)(2,1)S(1)}, u32[]{:S(2)}, u32[]{:S(2)}) %collective-permute-start.5) | collective-permute-done | bytes 131104 | tf_op jit(solution)/shard_map/ppermute | solution.py:147
  44.0 4.1 %collective-permute-done.6.after = bf16[256,256]{1,0:T(8,128)(2,1)S(1)} collective-permute-done((bf16[256,256]{1,0:T(8,128)(2,1)S(1)}, bf16[256,256]{1,0:T(8,128)(2,1)S(1)}, u32[]{:S(2)}, u32[]{:S(2)}) %collective-permute-start.6) | collective-permute-done | bytes 131104 | tf_op jit(solution)/shard_map/ppermute | solution.py:147
  48.1 2.6 %shard_map.98 = (f32[256,256]{1,0:T(8,128)S(1)}, f32[256,256]{1,0:T(8,128)S(1)}, bf16[256,256]{1,0:T(8,128)(2,1)}) custom-call(s32[14]{0:T(128)S(1)} %copy-done.5, s32[1,1]{1,0:T(1,128)S(6)} %copy.11.live, bf16[14,256,256]{2,1,0:T(8,128)(2,1)S(1)} %bitcast.19, bf16[14,256,256]{2,1,0:T(8,128)(2,1)S(1)} %collective-permute-done.2.right, ...), custom_call_target="tpu_custom_call" | custom-call | flops 100000000 | bytes 4456508 | tf_op jit(solution)/shard_map/pallas_call | solution.py:20
  51.1 15.2 %all_to_all.11 = f32[16,1,128]{2,1,0:T(1,128)S(1)} all-to-all(f32[16,1,128]{2,1,0:T(1,128)S(1)} %bitcast.24), channel_id=1, replica_groups=mesh['sec'=32,'blk'=16] {'blk'}, dimensions={0} | all-to-all | bytes 16384 | tf_op jit(solution)/shard_map/all_to_all | solution.py:167
  66.2 1.4 %shard_map.100 = (f32[256,256]{1,0:T(8,128)}, bf16[256,256]{1,0:T(8,128)(2,1)S(1)}, f32[1,128]{1,0:T(1,128)}) custom-call(f32[16,128]{1,0:T(8,128)S(1)} %bitcast.23, f32[256,256]{1,0:T(8,128)S(1)} %get-tuple-element.18.p.p0, f32[256,256]{1,0:T(8,128)S(1)} %get-tuple-element.24.p.p1, f32[256,256]{1,0:T(8,128)S(1)} %get-tuple-element.27.p.p2, ...), custom_call_target="tpu_custom_call" | custom-call | flops 100000000 | bytes 1056768 | tf_op jit(solution)/shard_map/pallas_call | solution.py:20
  67.6 3.1 %collective-permute-start.7 = (bf16[256,256]{1,0:T(8,128)(2,1)S(1)}, bf16[256,256]{1,0:T(8,128)(2,1)S(1)}, u32[]{:S(2)}, u32[]{:S(2)}) collective-permute-start(bf16[256,256]{1,0:T(8,128)(2,1)S(1)} %get-tuple-element.32), channel_id=1, source_target_pairs={{16,0},{32,16},{48,32},{64,48},{80,64},{96,80},{112,96},{128,112},... | collective-permute-start | bytes 393224 | tf_op jit(solution)/shard_map/ppermute | solution.py:171
  71.4 5.9 %collective-permute-done.7 = bf16[256,256]{1,0:T(8,128)(2,1)S(1)} collective-permute-done((bf16[256,256]{1,0:T(8,128)(2,1)S(1)}, bf16[256,256]{1,0:T(8,128)(2,1)S(1)}, u32[]{:S(2)}, u32[]{:S(2)}) %collective-permute-start.7) | collective-permute-done | bytes 131104 | tf_op jit(solution)/shard_map/ppermute | solution.py:171
  77.6 0.9 %fusion = f32[1,1,256,256]{3,2,1,0:T(8,128)} fusion(f32[256,256]{1,0:T(8,128)S(1)} %fusion.1, bf16[256,256]{1,0:T(8,128)(2,1)S(1)} %get-tuple-element.32, bf16[256]{0:T(256)(128)(2,1)S(1)} %compare_convert_fusion), kind=kOutput, calls=%fused_computation.1 | convolution fusion | flops 33685504 | bytes 655872 | tf_op jit(solution)/shard_map/dot_general | solution.py:36
  (17 shorter events, 2.7 us)
Async XLA Ops:
  0.6 26.4 %collective-permute-start.2 = (bf16[14,256,256]{2,1,0:T(8,128)(2,1)}, bf16[14,256,256]{2,1,0:T(8,128)(2,1)S(1)}, u32[]{:S(2)}, u32[]{:S(2)}) collective-permute-start(bf16[14,256,256]{2,1,0:T(8,128)(2,1)} %bitcast.26), channel_id=1, source_target_pairs={{16,0},{32,16},{48,32},{64,48},{80,64},{96,80},{112,96},{128,112},... | collective-permute-start | bytes 5505032 | tf_op jit(solution)/shard_map/ppermute | solution.py:142
  3.9 1.0 %copy-start.6 = (f32[1,1,256,256]{3,2,1,0:T(8,128)S(1)}, f32[1,1,256,256]{3,2,1,0:T(8,128)}, u32[]{:S(2)}) copy-start(f32[1,1,256,256]{3,2,1,0:T(8,128)} %param.10) | copy-start | bytes 786436
  4.9 5.9 %collective-permute-start = (bf16[256,256]{1,0:T(8,128)(2,1)S(1)}, bf16[256,256]{1,0:T(8,128)(2,1)S(1)}, u32[]{:S(2)}, u32[]{:S(2)}) collective-permute-start(bf16[256,256]{1,0:T(8,128)(2,1)S(1)} %get-tuple-element.19.own), channel_id=1, source_target_pairs={{0,1},{1,2},{2,3},{3,4},{4,5},{5,6},{6,7},{7,8},{8,9},{9,10},{10,1... | collective-permute-start | bytes 393224 | tf_op jit(solution)/shard_map/ppermute | solution.py:147
  8.0 6.7 %collective-permute-start.1 = (bf16[256,256]{1,0:T(8,128)(2,1)S(1)}, bf16[256,256]{1,0:T(8,128)(2,1)S(1)}, u32[]{:S(2)}, u32[]{:S(2)}) collective-permute-start(bf16[256,256]{1,0:T(8,128)(2,1)S(1)} %get-tuple-element.19.own), channel_id=1, source_target_pairs={{1,0},{2,1},{3,2},{4,3},{5,4},{6,5},{7,6},{8,7},{9,8},{10,9},{11,1... | collective-permute-start | bytes 393224 | tf_op jit(solution)/shard_map/ppermute | solution.py:147
  14.6 1.5 %copy-start = (bf16[1,14,1,256,256]{4,3,2,1,0:T(8,128)(2,1)S(1)}, bf16[1,14,1,256,256]{4,3,2,1,0:T(8,128)(2,1)}, u32[]{:S(2)}) copy-start(bf16[1,14,1,256,256]{4,3,2,1,0:T(8,128)(2,1)} %param.7) | copy-start | bytes 5505028
  16.1 0.9 %copy-start.2 = (bf16[1,1,256,256]{3,2,1,0:T(8,128)(2,1)S(1)}, bf16[1,1,256,256]{3,2,1,0:T(8,128)(2,1)}, u32[]{:S(2)}) copy-start(bf16[1,1,256,256]{3,2,1,0:T(8,128)(2,1)} %param.9) | copy-start | bytes 393220
  17.1 0.7 copy-start.4
  27.1 9.5 %copy-start.1 = (bf16[1,14,1,256,256]{4,3,2,1,0:T(8,128)(2,1)S(1)}, bf16[1,14,1,256,256]{4,3,2,1,0:T(8,128)(2,1)}, u32[]{:S(2)}) copy-start(bf16[1,14,1,256,256]{4,3,2,1,0:T(8,128)(2,1)} %param.7) | copy-start | bytes 5505028
  27.1 9.5 %copy-start.3 = (bf16[1,1,256,256]{3,2,1,0:T(8,128)(2,1)S(1)}, bf16[1,1,256,256]{3,2,1,0:T(8,128)(2,1)}, u32[]{:S(2)}) copy-start(bf16[1,1,256,256]{3,2,1,0:T(8,128)(2,1)} %param.9) | copy-start | bytes 393220
  27.1 9.5 %copy-start.5 = (s32[14]{0:T(128)S(1)}, s32[14]{0:T(128)}, u32[]{:S(2)}) copy-start(s32[14]{0:T(128)} %shift.5) | copy-start | bytes 172
  27.7 5.1 %collective-permute-start.3 = (bf16[256,256]{1,0:T(8,128)(2,1)S(1)}, bf16[256,256]{1,0:T(8,128)(2,1)S(1)}, u32[]{:S(2)}, u32[]{:S(2)}) collective-permute-start(bf16[256,256]{1,0:T(8,128)(2,1)S(1)} %get-tuple-element.23.own), channel_id=1, source_target_pairs={{0,1},{1,2},{2,3},{3,4},{4,5},{5,6},{6,7},{7,8},{8,9},{9,10},{10,1... | collective-permute-start | bytes 393224 | tf_op jit(solution)/shard_map/ppermute | solution.py:147
  30.9 5.7 %collective-permute-start.4 = (bf16[256,256]{1,0:T(8,128)(2,1)S(1)}, bf16[256,256]{1,0:T(8,128)(2,1)S(1)}, u32[]{:S(2)}, u32[]{:S(2)}) collective-permute-start(bf16[256,256]{1,0:T(8,128)(2,1)S(1)} %get-tuple-element.23.own), channel_id=1, source_target_pairs={{1,0},{2,1},{3,2},{4,3},{5,4},{6,5},{7,6},{8,7},{9,8},{10,9},{11,1... | collective-permute-start | bytes 393224 | tf_op jit(solution)/shard_map/ppermute | solution.py:147
  38.5 5.5 %collective-permute-start.5 = (bf16[256,256]{1,0:T(8,128)(2,1)S(1)}, bf16[256,256]{1,0:T(8,128)(2,1)S(1)}, u32[]{:S(2)}, u32[]{:S(2)}) collective-permute-start(bf16[256,256]{1,0:T(8,128)(2,1)S(1)} %get-tuple-element.26.own), channel_id=1, source_target_pairs={{0,1},{1,2},{2,3},{3,4},{4,5},{5,6},{6,7},{7,8},{8,9},{9,10},{10,1... | collective-permute-start | bytes 393224 | tf_op jit(solution)/shard_map/ppermute | solution.py:147
  41.6 6.5 %collective-permute-start.6 = (bf16[256,256]{1,0:T(8,128)(2,1)S(1)}, bf16[256,256]{1,0:T(8,128)(2,1)S(1)}, u32[]{:S(2)}, u32[]{:S(2)}) collective-permute-start(bf16[256,256]{1,0:T(8,128)(2,1)S(1)} %get-tuple-element.26.own), channel_id=1, source_target_pairs={{1,0},{2,1},{3,2},{4,3},{5,4},{6,5},{7,6},{8,7},{9,8},{10,9},{11,1... | collective-permute-start | bytes 393224 | tf_op jit(solution)/shard_map/ppermute | solution.py:147
  67.6 9.7 %collective-permute-start.7 = (bf16[256,256]{1,0:T(8,128)(2,1)S(1)}, bf16[256,256]{1,0:T(8,128)(2,1)S(1)}, u32[]{:S(2)}, u32[]{:S(2)}) collective-permute-start(bf16[256,256]{1,0:T(8,128)(2,1)S(1)} %get-tuple-element.32), channel_id=1, source_target_pairs={{16,0},{32,16},{48,32},{64,48},{80,64},{96,80},{112,96},{128,112},... | collective-permute-start | bytes 393224 | tf_op jit(solution)/shard_map/ppermute | solution.py:171

commit v2 on v1

v2 whole, which is shorter than its diff:
```python
import jax
import jax.numpy as jnp
from jax import lax
from jax.experimental import pallas as pl
from jax.experimental.pallas import tpu as pltpu
from jax.sharding import PartitionSpec as P


STEP = 0.3
VM = pl.BlockSpec(memory_space=pltpu.VMEM)
SM = pl.BlockSpec(memory_space=pltpu.SMEM)
F32 = jnp.float32
BF = jnp.bfloat16
LIMIT = 20 * 1024 * 1024


def call(body, outs, args, specs, scratch=(), flops=10**8, out_specs=None):
    moved = sum(a.size * a.dtype.itemsize for a in args)
    return pl.pallas_call(
        body,
        out_shape=[jax.ShapeDtypeStruct(s, d) for s, d in outs],
        in_specs=specs,
        out_specs=out_specs or [VM] * len(outs),
        scratch_shapes=list(scratch),
        compiler_params=pltpu.CompilerParams(vmem_limit_bytes=LIMIT),
        cost_estimate=pl.CostEstimate(flops=flops, bytes_accessed=moved, transcendentals=0),
    )(*args)


def dot(a, b):
    return jnp.dot(a, b, preferred_element_type=F32)


def dot_t(a, b):
    return lax.dot_general(a, b, (((1,), (1,)), ((), ())), preferred_element_type=F32)


def inside(live, shape):
    rows = lax.broadcasted_iota(jnp.int32, shape, 0)
    cols = lax.broadcasted_iota(jnp.int32, shape, 1)
    return (rows < live) & (cols < live)


def init_body(live, start, p_ref, h_ref):
    p = jnp.where(inside(live[0, 0], start.shape), start[...], 0.0)
    p_ref[...] = p
    h_ref[...] = p.astype(BF)


def fill(hs, own, near, far):
    hs[0] = own[...]
    hs[1] = near[...]
    hs[2] = far[...]


def inner_body(slot, left, own, near, far, onsite, inner, total, hs):
    fill(hs, own, near, far)
    h = own[...]
    total[...] = dot(onsite[...], h) + dot_t(h, onsite[...])
    for k in range(left.shape[0]):
        inner[k] = dot(left[k], hs[slot[k]]).astype(BF)


def finish(total, live, p, w_ref, p_ref, h_ref):
    w = jnp.where(inside(live, total.shape), total[...], 0.0)
    w_ref[...] = w
    q = p - STEP * w
    p_ref[...] = q
    h_ref[...] = q.astype(BF)


def outer_sum(inner, right, start):
    total = start[...]
    for k in range(right.shape[0]):
        total = total + dot_t(inner[k], right[k])
    return total


def load_body(left_hbm, onsite_hbm, left, onsite, sem):
    copies = [
        pltpu.make_async_copy(left_hbm, left, sem.at[0]),
        pltpu.make_async_copy(onsite_hbm, onsite, sem.at[1]),
    ]
    for copy in copies:
        copy.start()
    for copy in copies:
        copy.wait()


def even_body(slot, live, inner, right_hbm, start, p, w_ref, p_ref, h_ref, right, sem):
    @pl.when(slot[right.shape[0]] == 0)
    def _():
        terms = right.shape[0]
        copies = [pltpu.make_async_copy(right_hbm.at[k], right.at[k], sem.at[k]) for k in range(terms)]
        for copy in copies:
            copy.start()
        total = start[...]
        for k in range(terms):
            copies[k].wait()
            total = total + dot_t(inner[k], right[k])
        finish(total, live[0, 0], p[...], w_ref, p_ref, h_ref)


def odd_body(slot, live, inner, right, start, p, _, __, w_ref, p_ref, h_ref):
    @pl.when(slot[right.shape[0]] == 1)
    def _():
        finish(outer_sum(inner, right, start), live[0, 0], p[...], w_ref, p_ref, h_ref)


def product(slot, left, right, own, near, far, onsite, hs):
    fill(hs, own, near, far)
    h = own[...]
    total = dot(onsite[...], h) + dot_t(h, onsite[...])
    for k in range(left.shape[0]):
        part = dot(left[k], hs[slot[k]]).astype(BF)
        total = total + dot_t(part, right[k])
    return total


def both_body(slot, live, left, onsite, *refs):
    sets, (w_ref, p_ref, h_ref, old_w, old_p, hs) = (refs[:6], refs[6:12]), refs[12:]
    for turn, (right, own, near, far, p, w) in enumerate(sets):

        @pl.when(slot[left.shape[0]] == turn)
        def _():
            total = product(slot, left, right, own, near, far, onsite, hs)
            finish(total, live[0, 0], p[...], w_ref, p_ref, h_ref)
            old_w[...] = w[...]
            old_p[...] = p[...]


def put(out, base, pairs):
    lane = lax.broadcasted_iota(jnp.int32, out.shape, 1)
    for i, (x, y) in enumerate(pairs):
        out = jnp.where(lane == base + i, jnp.sum(x * y), out)
    return out


def gram_body(p0, w0, w1, g_ref):
    a, b, c = p0[...], w0[...], w1[...]
    pairs = ((a, a), (a, b), (a, c), (b, b), (b, c), (c, c))
    g_ref[...] = put(jnp.zeros(g_ref.shape, F32), 0, pairs)


def last_body(slot, live, left, right_even, right_odd, own, near, far, onsite, p, p0, w0, w1, g, p_ref, g_ref, hs):
    for turn, right in enumerate((right_even, right_odd)):

        @pl.when(slot[left.shape[0]] == turn)
        def _():
            total = product(slot, left, right, own, near, far, onsite, hs)
            w = jnp.where(inside(live[0, 0], total.shape), total, 0.0)
            p_ref[...] = p[...] - STEP * w
            g_ref[...] = put(g[...], 6, ((p0[...], w), (w0[...], w), (w1[...], w), (w, w)))


def coef_body(parts, p0, p1, p2, p3, half_ref, coef_ref):
    sums = jnp.sum(parts[...], axis=0, keepdims=True)
    v = [sums[:, i : i + 1] for i in range(10)]
    weight, p0w = v[0], [v[1], v[2], v[6]]
    ww = [[v[3], v[4], v[7]], [v[4], v[5], v[8]], [v[7], v[8], v[9]]]
    p1w = [p0w[j] - STEP * ww[0][j] for j in range(3)]
    p2w = [p1w[j] - STEP * ww[1][j] for j in range(3)]
    pw = [p0w, p1w, p2w]
    one = jnp.ones_like(weight)
    coef, scale = [one], one
    energy = one
    for n in range(3):
        c = jnp.zeros_like(one)
        a = jnp.zeros_like(one)
        for i in range(n + 1):
            for j in range(n + 1):
                t = coef[i] * coef[j]
                c = c + t * pw[i][j]
                a = a + t * ww[i][j]
        energy = c * scale / weight
        excess = jnp.maximum(a * scale / weight - energy * energy, 0.0)
        scale = scale / (1.0 + STEP * STEP * excess)
        g = STEP * energy
        coef = [g * coef[0]] + [coef[i - 1] + g * coef[i] for i in range(1, n + 1)] + [one]
    root = jnp.sqrt(scale)
    coef = [root * c for c in coef]
    theta = coef[0] * p0[...] + coef[1] * p1[...] + coef[2] * p2[...] + coef[3] * p3[...]
    half_ref[...] = theta.astype(BF)
    row = lax.broadcasted_iota(jnp.int32, coef_ref.shape, 0)
    out = jnp.broadcast_to(energy, coef_ref.shape)
    for i, c in enumerate(coef):
        out = jnp.where(row == i, c, out)
    coef_ref[...] = out


def theta_body(coef, p0, p1, p2, p3, theta_ref):
    c = [coef[i : i + 1, 0:1] for i in range(4)]
    theta_ref[...] = c[0] * p0[...] + c[1] * p1[...] + c[2] * p2[...] + c[3] * p3[...]


def own_body(rank, half, own_ref):
    h = half[...]
    cols = lax.broadcasted_iota(jnp.int32, h.shape, 1)
    own_ref[...] = dot_t(jnp.where(cols < rank[0, 0], h, jnp.zeros_like(h)), h)


def density_body(rank, beside, own, out_ref):
    b = beside[...]
    rows = lax.broadcasted_iota(jnp.int32, b.shape, 0)
    kept = jnp.where(rows < rank[0, 0], b, jnp.zeros_like(b))
    other = lax.dot_general(kept, b, (((0,), (0,)), ((), ())), preferred_element_type=F32)
    out_ref[...] = own[...] + other


def section_step(left_env, right_out, onsite, start_state, live, rank, shift):
    terms, width = left_env.shape[1], left_env.shape[-1]
    square = (width, width)
    left = left_env.reshape(terms, *square)
    onsite = onsite.reshape(square)
    sections, blocks = lax.axis_size("sec"), lax.axis_size("blk")
    sec, blk = lax.axis_index("sec"), lax.axis_index("blk")
    ahead = [(i + 1, i) for i in range(sections - 1)]
    near_pairs = [(i, i ^ 1) for i in range(blocks) if i ^ 1 < blocks]
    far_pairs = [(i, (i - 1 ^ 1) + 1) for i in range(1, blocks) if (i - 1 ^ 1) + 1 < blocks]
    near_shift = 1 - 2 * (blk % 2)
    slot = jnp.where(shift == 0, 0, jnp.where(shift == near_shift, 1, 2)).astype(jnp.int32)
    slot = jnp.concatenate([slot, jnp.full((1,), sec % 2, jnp.int32)])
    built = right_out.reshape(terms, *square)
    right_odd = lax.ppermute(built, "sec", ahead[1::2])
    state = start_state.reshape(square)
    p0, h0 = call(init_body, [(square, F32), (square, BF)], (live, state), [SM, VM])
    hbm = pl.BlockSpec(memory_space=pl.ANY)
    outs = [((terms, *square), BF), (square, BF)]
    sems = [pltpu.SemaphoreType.DMA((2,))]
    left, onsite = call(load_body, outs, (left, onsite), [hbm, hbm], sems)

    def halo(h, which):
        def pairs(base):
            return [(s * blocks + i, s * blocks + j) for s in which for i, j in base]

        axes = ("sec", "blk")
        near = lax.ppermute(h, axes, pairs(near_pairs))
        far = lax.ppermute(h, axes, pairs(far_pairs))
        return near, far

    every = range(sections)
    triple = [(square, F32), (square, F32), (square, BF)]
    slots = [pltpu.VMEM((3, *square), BF)]
    near, far = halo(h0, every)
    right_even = lax.ppermute(built, "sec", ahead[0::2])
    inner, total = call(
        inner_body,
        [((terms, *square), BF), (square, F32)],
        (slot, left, h0, near, far, onsite),
        [SM] + [VM] * 5,
        slots,
    )
    args = (slot, live, inner, right_even, total, p0)
    specs = [SM, SM, VM, hbm, VM, VM]
    outs = triple + [((terms, *square), BF)]
    w0, p1, h1, right_even = call(even_body, outs, args, specs, [pltpu.SemaphoreType.DMA((terms,))])
    near, far = halo(h1, every[0::2])
    sets = [right_even, h1, near, far, p1, w0]
    args = (slot, live, inner, right_odd, total, p0, near, far)
    w0, p1, h1 = call(odd_body, triple, args, [SM, SM] + [VM] * 4 + [hbm] * 2)
    sets += [right_odd, h1, *halo(h1, every[1::2]), p1, w0]
    outs = triple + [(square, F32)] * 2
    w1, p2, h2, w0, p1 = call(both_body, outs, (slot, live, left, onsite, *sets), [SM, SM] + [VM] * 14, slots)
    table = (blocks, 128)
    (gram,) = call(gram_body, [(table, F32)], (p0, w0, w1), [VM] * 3)
    args = (slot, live, left, right_even, right_odd, h2, *halo(h2, every), onsite, p2, p0, w0, w1, gram)
    p3, gram = call(last_body, [(square, F32), (table, F32)], args, [SM, SM] + [VM] * 12, slots)
    parts = lax.all_to_all(gram, "blk", 0, 0, tiled=True)
    half, coef = call(coef_body, [(square, BF), ((8, 128), F32)], (parts, p0, p1, p2, p3), [VM] * 5)
    beside = lax.ppermute(half, "sec", ahead)
    (theta,) = call(theta_body, [(square, F32)], (coef, p0, p1, p2, p3), [VM] * 5)
    (own,) = call(own_body, [(square, F32)], (rank, half), [SM, VM])
    (density,) = call(density_body, [(square, F32)], (rank, beside, own), [SM, VM, VM])
    return theta[None, None], coef[4, :1], density[None, None]


def solution(mesh):
    placed = (
        P("sec", None, "blk", None, None),
        P("sec", None, "blk", None, None),
        P("sec", "blk", None, None),
        P("sec", "blk", None, None),
        P("sec", "blk"),
        P("sec", "blk"),
        P(),
    )
    return jax.shard_map(
        section_step,
        mesh=mesh,
        in_specs=placed,
        out_specs=(P("sec", "blk", None, None), P("sec"), P("sec", "blk", None, None)),
        check_vma=False,
    )
```

time: 79 us -> 78 us (0.987)
  waiting for transfers between devices: 28.9 us -> 19 us
  blocking collectives: 15.2 us -> 19 us
  starting transfers between devices: 18.9 us -> 22.3 us
  Pallas kernels: 8.23 us -> 10.5 us
  matrix products: 1.24 us -> 0 us
    ppermute x8 -> x11, waiting for transfers between devices: 28.9 us -> 19 us  [the longest x1 12.4 us: section_step(): right_odd = lax.ppermute(built, 'sec', ahead[1::2])]
    all_to_all x1, blocking collectives: 15.2 us -> 19 us  [section_step(): parts = lax.all_to_all(gram, 'blk', 0, 0, tiled=True)]
    ppermute x8 -> x11, starting transfers between devices: 18.9 us -> 22.3 us  [the longest x4 12.6 us: halo(): near = lax.ppermute(h, axes, pairs(near_pairs))]
    pallas_call x7 -> x12, Pallas kernels: 8.23 us -> 10.5 us  [call(): pl.pallas_call(body, out_shape=[jax.ShapeDtypeStruct(s, d) for s, d in ou...]
    dot_general x2 -> x0, matrix products: 1.24 us -> none  [the longest x1 0.93 us: dot_t(): lax.dot_general(a, b, (((1,), (1,)), ((), ())), preferred_element_type=F32)]
    unnamed x14 -> x6, local copies, waits for them, and re-layouts: 4.01 us -> 3.35 us
  transfers between devices with their start and end apart: 8 -> 11, of which waited for: 8 -> 4; matrix products, arithmetic and copies ran while one was open for 0% -> 2% of each run, Pallas kernels for 2% -> 5%
where the time goes in v2:
time: 78 us; the launch traced here: 77.6 us
  starting transfers between devices  22.3 us (29%)
  waiting for transfers between devices  19 us (24%)
  blocking collectives  19 us (24%)
  Pallas kernels  10.5 us (13%)
  local copies, waits for them, and re-layouts  3.86 us (5%)
  between operations  2.11 us (3%)
    all_to_all x1, blocking collectives, section_step(): parts = lax.all_to_all(gram, 'blk', 0, 0, tiled=True)  19 us
    ppermute x4, starting transfers between devices, halo(): near = lax.ppermute(h, axes, pairs(near_pairs))  12.6 us
    ppermute x1, waiting for transfers between devices, section_step(): right_odd = lax.ppermute(built, 'sec', ahead[1::2])  12.4 us
    pallas_call x12, Pallas kernels, call(): pl.pallas_call(body, out_shape=[jax.ShapeDtypeStruct(s, d) for s, d in ou...  10.5 us
    ppermute x1, starting transfers between devices, section_step(): right_even = lax.ppermute(built, 'sec', ahead[0::2])  3.85 us
    unnamed x6, local copies, waits for them, and re-layouts  3.35 us
    ppermute x1, waiting for transfers between devices, section_step(): beside = lax.ppermute(half, 'sec', ahead)  3.34 us
    ppermute x4, waiting for transfers between devices, halo(): near = lax.ppermute(h, axes, pairs(near_pairs))  3.3 us
  transfers between devices with their start and end apart: 11, of which 4 were waited for; matrix products, arithmetic and copies ran while one was open for 2% of the time, Pallas kernels for 5%

profile of v2, /device:TPU:97, one launch (start us, length us, event | category | flops | bytes accessed | tf_op | source)
XLA Modules:
  0.0 77.6 jit_solution(17135371913243791922)
XLA Ops:
  0.6 3.9 %collective-permute-start.2 = (bf16[14,256,256]{2,1,0:T(8,128)(2,1)}, bf16[14,256,256]{2,1,0:T(8,128)(2,1)}, u32[]{:S(2)}, u32[]{:S(2)}) collective-permute-start(bf16[14,256,256]{2,1,0:T(8,128)(2,1)} %bitcast.19), channel_id=1, source_target_pairs={{16,0},{48,32},{80,64},{112,96},{144,128},{176,160},{208,192},{240... | collective-permute-start | bytes 5505032 | tf_op jit(solution)/shard_map/ppermute | solution.py:245
  4.5 1.3 %collective-permute-start.3 = (bf16[14,256,256]{2,1,0:T(8,128)(2,1)}, bf16[14,256,256]{2,1,0:T(8,128)(2,1)S(1)}, u32[]{:S(2)}, u32[]{:S(2)}) collective-permute-start(bf16[14,256,256]{2,1,0:T(8,128)(2,1)} %bitcast.20), channel_id=1, source_target_pairs={{32,16},{64,48},{96,80},{128,112},{160,144},{192,176},{224,208},{2... | collective-permute-start | bytes 5505032 | tf_op jit(solution)/shard_map/ppermute | solution.py:224
  6.4 0.9 %copy-done.2 = f32[1,1,256,256]{3,2,1,0:T(8,128)S(1)} copy-done((f32[1,1,256,256]{3,2,1,0:T(8,128)S(1)}, f32[1,1,256,256]{3,2,1,0:T(8,128)}, u32[]{:S(2)}) %copy-start.2) | copy-done | bytes 262168
  7.4 3.1 %collective-permute-start = (bf16[256,256]{1,0:T(8,128)(2,1)S(1)}, bf16[256,256]{1,0:T(8,128)(2,1)S(1)}, u32[]{:S(2)}, u32[]{:S(2)}) collective-permute-start(bf16[256,256]{1,0:T(8,128)(2,1)S(1)} %get-tuple-element.26.own), channel_id=1, source_target_pairs={{0,1},{1,0},{2,3},{3,2},{4,5},{5,4},{6,7},{7,6},{8,9},{9,8},{10,11... | collective-permute-start | bytes 393224 | tf_op jit(solution)/shard_map/ppermute | solution.py:237
  10.5 0.7 collective-permute-start.1
  11.9 1.5 %copy-done = bf16[1,14,1,256,256]{4,3,2,1,0:T(8,128)(2,1)S(1)} copy-done((bf16[1,14,1,256,256]{4,3,2,1,0:T(8,128)(2,1)S(1)}, bf16[1,14,1,256,256]{4,3,2,1,0:T(8,128)(2,1)}, u32[]{:S(2)}) %copy-start) | copy-done | bytes 1835032
  13.4 0.9 %copy-done.1 = bf16[1,1,256,256]{3,2,1,0:T(8,128)(2,1)S(1)} copy-done((bf16[1,1,256,256]{3,2,1,0:T(8,128)(2,1)S(1)}, bf16[1,1,256,256]{3,2,1,0:T(8,128)(2,1)}, u32[]{:S(2)}) %copy-start.1) | copy-done | bytes 131096
  14.7 1.3 %shard_map.96 = (bf16[14,256,256]{2,1,0:T(8,128)(2,1)S(1)}, f32[256,256]{1,0:T(8,128)S(1)}) custom-call(s32[15]{0:T(128)S(1)} %pad_add_fusion.slot, bf16[14,256,256]{2,1,0:T(8,128)(2,1)S(1)} %get-tuple-element.25.left, bf16[256,256]{1,0:T(8,128)(2,1)S(1)} %get-tuple-element.26.own, bf16[256,256]{1,0:T(8,128)(2,1)S(1)} %collective-permute-done.near, ...), custom_call_target="tpu_custom_call" | custom-call | flops 100000000 | bytes 2359356 | tf_op jit(solution)/shard_map/pallas_call | solution.py:19
  16.0 0.7 shard_map.97
  18.0 12.4 %collective-permute-done.3.right.refs_6_.right_odd = bf16[14,256,256]{2,1,0:T(8,128)(2,1)S(1)} collective-permute-done((bf16[14,256,256]{2,1,0:T(8,128)(2,1)}, bf16[14,256,256]{2,1,0:T(8,128)(2,1)S(1)}, u32[]{:S(2)}, u32[]{:S(2)}) %collective-permute-start.3) | collective-permute-done | bytes 1835040 | tf_op jit(solution)/shard_map/ppermute | solution.py:224
  30.4 1.2 %shard_map.98 = (f32[256,256]{1,0:T(8,128)S(1)}, f32[256,256]{1,0:T(8,128)S(1)}, bf16[256,256]{1,0:T(8,128)(2,1)S(1)}) custom-call(s32[15]{0:T(128)S(1)} %pad_add_fusion.slot, s32[1,1]{1,0:T(1,128)S(6)} %copy.11.live, bf16[14,256,256]{2,1,0:T(8,128)(2,1)S(1)} %get-tuple-element.28.inner, ...), custom_call_target="tpu_custom_call" | custom-call | flops 100000000 | bytes 4456512 | tf_op jit(solution)/shard_map/pallas_call | solution.py:19
  31.7 3.1 %collective-permute-start.6 = (bf16[256,256]{1,0:T(8,128)(2,1)S(1)}, bf16[256,256]{1,0:T(8,128)(2,1)S(1)}, u32[]{:S(2)}, u32[]{:S(2)}) collective-permute-start(bf16[256,256]{1,0:T(8,128)(2,1)S(1)} %get-tuple-element.35.refs_7_), channel_id=1, source_target_pairs={{16,17},{17,16},{18,19},{19,18},{20,21},{21,20},{22,23},{23,22},{2... | collective-permute-start | bytes 393224 | tf_op jit(solution)/shard_map/ppermute | solution.py:237
  34.8 0.7 collective-permute-start.7
  35.5 1.9 %collective-permute-done.6.refs_8_ = bf16[256,256]{1,0:T(8,128)(2,1)S(1)} collective-permute-done((bf16[256,256]{1,0:T(8,128)(2,1)S(1)}, bf16[256,256]{1,0:T(8,128)(2,1)S(1)}, u32[]{:S(2)}, u32[]{:S(2)}) %collective-permute-start.6) | collective-permute-done | bytes 131104 | tf_op jit(solution)/shard_map/ppermute | solution.py:237
  37.4 1.9 %shard_map.99 = (f32[256,256]{1,0:T(8,128)S(1)}, f32[256,256]{1,0:T(8,128)S(1)}, bf16[256,256]{1,0:T(8,128)(2,1)S(1)}, f32[256,256]{1,0:T(8,128)S(1)}, f32[256,256]{1,0:T(8,128)S(1)}) custom-call(s32[15]{0:T(128)S(1)} %pad_add_fusion.slot, s32[1,1]{1,0:T(1,128)S(6)} %copy.11.live, bf16[14,256,256]{2,1,0:T(8,128)(2,1)S(1)} %get-tuple-element.25.left, ...), custom_call_target="tpu_custom_call" | custom-call | flops 100000000 | bytes 7471168 | tf_op jit(solution)/shard_map/pallas_call | solution.py:19
  39.3 5.7 %collective-permute-start.8 = (bf16[256,256]{1,0:T(8,128)(2,1)S(1)}, bf16[256,256]{1,0:T(8,128)(2,1)S(1)}, u32[]{:S(2)}, u32[]{:S(2)}) collective-permute-start(bf16[256,256]{1,0:T(8,128)(2,1)S(1)} %get-tuple-element.38.own), channel_id=1, source_target_pairs={{0,1},{1,0},{2,3},{3,2},{4,5},{5,4},{6,7},{7,6},{8,9},{9,8},{10,11... | collective-permute-start | bytes 393224 | tf_op jit(solution)/shard_map/ppermute | solution.py:237
  46.0 1.4 %collective-permute-done.8.near = bf16[256,256]{1,0:T(8,128)(2,1)S(1)} collective-permute-done((bf16[256,256]{1,0:T(8,128)(2,1)S(1)}, bf16[256,256]{1,0:T(8,128)(2,1)S(1)}, u32[]{:S(2)}, u32[]{:S(2)}) %collective-permute-start.8) | collective-permute-done | bytes 131104 | tf_op jit(solution)/shard_map/ppermute | solution.py:237
  47.4 2.1 %shard_map.101 = (f32[256,256]{1,0:T(8,128)S(1)}, f32[16,128]{1,0:T(8,128)S(1)}) custom-call(s32[15]{0:T(128)S(1)} %pad_add_fusion.slot, s32[1,1]{1,0:T(1,128)S(6)} %copy.11.live, bf16[14,256,256]{2,1,0:T(8,128)(2,1)S(1)} %get-tuple-element.25.left, bf16[14,256,256]{2,1,0:T(8,128)(2,1)S(1)} %get-tuple-element.31.refs_0_.right_even, ...), custom_call_target="tpu_custom_call" | custom-call | flops 100000000 | bytes 7086144 | tf_op jit(solution)/shard_map/pallas_call | solution.py:19
  49.5 19.0 %all_to_all.11 = f32[16,1,128]{2,1,0:T(1,128)S(1)} all-to-all(f32[16,1,128]{2,1,0:T(1,128)S(1)} %bitcast.15), channel_id=1, replica_groups=mesh['sec'=32,'blk'=16] {'blk'}, dimensions={0} | all-to-all | bytes 16384 | tf_op jit(solution)/shard_map/all_to_all | solution.py:268
  68.4 0.7 shard_map.102
  69.1 1.9 %collective-permute-start.10 = (bf16[256,256]{1,0:T(8,128)(2,1)S(1)}, bf16[256,256]{1,0:T(8,128)(2,1)S(1)}, u32[]{:S(2)}, u32[]{:S(2)}) collective-permute-start(bf16[256,256]{1,0:T(8,128)(2,1)S(1)} %get-tuple-element.46.half), channel_id=1, source_target_pairs={{16,0},{32,16},{48,32},{64,48},{80,64},{96,80},{112,96},{128,112},... | collective-permute-start | bytes 393224 | tf_op jit(solution)/shard_map/ppermute | solution.py:270
  72.2 0.8 %shard_map.103 = f32[256,256]{1,0:T(8,128)} custom-call(f32[8,128]{1,0:T(8,128)S(1)} %get-tuple-element.45.coef, f32[256,256]{1,0:T(8,128)S(1)} %get-tuple-element.30.p.p0, f32[256,256]{1,0:T(8,128)S(1)} %get-tuple-element.43.p1, f32[256,256]{1,0:T(8,128)S(1)} %get-tuple-element.39.p.p2, f32[256,256]{1,0:T(8,128)S(1)} %get-tuple-element.44.p3), custom_call_target="tpu_custom_call" | custom-call | flops 100000000 | bytes 1052672 | tf_op jit(solution)/shard_map/pallas_call | solution.py:19
  73.3 3.3 %collective-permute-done.10.beside = bf16[256,256]{1,0:T(8,128)(2,1)S(1)} collective-permute-done((bf16[256,256]{1,0:T(8,128)(2,1)S(1)}, bf16[256,256]{1,0:T(8,128)(2,1)S(1)}, u32[]{:S(2)}, u32[]{:S(2)}) %collective-permute-start.10) | collective-permute-done | bytes 131104 | tf_op jit(solution)/shard_map/ppermute | solution.py:270
  76.6 0.9 %shard_map.105 = f32[256,256]{1,0:T(8,128)} custom-call(s32[1,1]{1,0:T(1,128)S(6)} %copy.12.rank, bf16[256,256]{1,0:T(8,128)(2,1)S(1)} %collective-permute-done.10.beside, f32[256,256]{1,0:T(8,128)S(1)} %shard_map.104.own), custom_call_target="tpu_custom_call" | custom-call | flops 100000000 | bytes 393220 | tf_op jit(solution)/shard_map/pallas_call | solution.py:19
  (20 shorter events, 4.1 us)
Async XLA Ops:
  0.6 15.4 %collective-permute-start.2 = (bf16[14,256,256]{2,1,0:T(8,128)(2,1)}, bf16[14,256,256]{2,1,0:T(8,128)(2,1)}, u32[]{:S(2)}, u32[]{:S(2)}) collective-permute-start(bf16[14,256,256]{2,1,0:T(8,128)(2,1)} %bitcast.19), channel_id=1, source_target_pairs={{16,0},{48,32},{80,64},{112,96},{144,128},{176,160},{208,192},{240... | collective-permute-start | bytes 5505032 | tf_op jit(solution)/shard_map/ppermute | solution.py:245
  4.5 26.0 %collective-permute-start.3 = (bf16[14,256,256]{2,1,0:T(8,128)(2,1)}, bf16[14,256,256]{2,1,0:T(8,128)(2,1)S(1)}, u32[]{:S(2)}, u32[]{:S(2)}) collective-permute-start(bf16[14,256,256]{2,1,0:T(8,128)(2,1)} %bitcast.20), channel_id=1, source_target_pairs={{32,16},{64,48},{96,80},{128,112},{160,144},{192,176},{224,208},{2... | collective-permute-start | bytes 5505032 | tf_op jit(solution)/shard_map/ppermute | solution.py:224
  6.4 1.0 %copy-start.2 = (f32[1,1,256,256]{3,2,1,0:T(8,128)S(1)}, f32[1,1,256,256]{3,2,1,0:T(8,128)}, u32[]{:S(2)}) copy-start(f32[1,1,256,256]{3,2,1,0:T(8,128)} %param.10) | copy-start | bytes 786436
  7.4 7.3 %collective-permute-start = (bf16[256,256]{1,0:T(8,128)(2,1)S(1)}, bf16[256,256]{1,0:T(8,128)(2,1)S(1)}, u32[]{:S(2)}, u32[]{:S(2)}) collective-permute-start(bf16[256,256]{1,0:T(8,128)(2,1)S(1)} %get-tuple-element.26.own), channel_id=1, source_target_pairs={{0,1},{1,0},{2,3},{3,2},{4,5},{5,4},{6,7},{7,6},{8,9},{9,8},{10,11... | collective-permute-start | bytes 393224 | tf_op jit(solution)/shard_map/ppermute | solution.py:237
  10.5 4.2 %collective-permute-start.1 = (bf16[256,256]{1,0:T(8,128)(2,1)S(1)}, bf16[256,256]{1,0:T(8,128)(2,1)S(1)}, u32[]{:S(2)}, u32[]{:S(2)}) collective-permute-start(bf16[256,256]{1,0:T(8,128)(2,1)S(1)} %get-tuple-element.26.own), channel_id=1, source_target_pairs={{1,2},{2,1},{3,4},{4,3},{5,6},{6,5},{7,8},{8,7},{9,10},{10,9},{11,... | collective-permute-start | bytes 393224 | tf_op jit(solution)/shard_map/ppermute | solution.py:238
  11.9 1.5 %copy-start = (bf16[1,14,1,256,256]{4,3,2,1,0:T(8,128)(2,1)S(1)}, bf16[1,14,1,256,256]{4,3,2,1,0:T(8,128)(2,1)}, u32[]{:S(2)}) copy-start(bf16[1,14,1,256,256]{4,3,2,1,0:T(8,128)(2,1)} %param.7) | copy-start | bytes 5505028
  13.4 0.9 %copy-start.1 = (bf16[1,1,256,256]{3,2,1,0:T(8,128)(2,1)S(1)}, bf16[1,1,256,256]{3,2,1,0:T(8,128)(2,1)}, u32[]{:S(2)}) copy-start(bf16[1,1,256,256]{3,2,1,0:T(8,128)(2,1)} %param.9) | copy-start | bytes 393220
  16.7 13.7 %collective-permute-start.4 = (bf16[256,256]{1,0:T(8,128)(2,1)S(1)}, bf16[256,256]{1,0:T(8,128)(2,1)S(1)}, u32[]{:S(2)}, u32[]{:S(2)}) collective-permute-start(bf16[256,256]{1,0:T(8,128)(2,1)S(1)} %get-tuple-element.32.refs_1_), channel_id=1, source_target_pairs={{0,1},{1,0},{2,3},{3,2},{4,5},{5,4},{6,7},{7,6},{8,9},{9,8},{10,11... | collective-permute-start | bytes 393224 | tf_op jit(solution)/shard_map/ppermute | solution.py:237
  17.4 13.1 %collective-permute-start.5 = (bf16[256,256]{1,0:T(8,128)(2,1)S(1)}, bf16[256,256]{1,0:T(8,128)(2,1)S(1)}, u32[]{:S(2)}, u32[]{:S(2)}) collective-permute-start(bf16[256,256]{1,0:T(8,128)(2,1)S(1)} %get-tuple-element.32.refs_1_), channel_id=1, source_target_pairs={{1,2},{2,1},{3,4},{4,3},{5,6},{6,5},{7,8},{8,7},{9,10},{10,9},{11,... | collective-permute-start | bytes 393224 | tf_op jit(solution)/shard_map/ppermute | solution.py:238
  31.7 5.7 %collective-permute-start.6 = (bf16[256,256]{1,0:T(8,128)(2,1)S(1)}, bf16[256,256]{1,0:T(8,128)(2,1)S(1)}, u32[]{:S(2)}, u32[]{:S(2)}) collective-permute-start(bf16[256,256]{1,0:T(8,128)(2,1)S(1)} %get-tuple-element.35.refs_7_), channel_id=1, source_target_pairs={{16,17},{17,16},{18,19},{19,18},{20,21},{21,20},{22,23},{23,22},{2... | collective-permute-start | bytes 393224 | tf_op jit(solution)/shard_map/ppermute | solution.py:237
  34.8 2.6 %collective-permute-start.7 = (bf16[256,256]{1,0:T(8,128)(2,1)S(1)}, bf16[256,256]{1,0:T(8,128)(2,1)S(1)}, u32[]{:S(2)}, u32[]{:S(2)}) collective-permute-start(bf16[256,256]{1,0:T(8,128)(2,1)S(1)} %get-tuple-element.35.refs_7_), channel_id=1, source_target_pairs={{17,18},{18,17},{19,20},{20,19},{21,22},{22,21},{23,24},{24,23},{2... | collective-permute-start | bytes 393224 | tf_op jit(solution)/shard_map/ppermute | solution.py:238
  39.3 8.1 %collective-permute-start.8 = (bf16[256,256]{1,0:T(8,128)(2,1)S(1)}, bf16[256,256]{1,0:T(8,128)(2,1)S(1)}, u32[]{:S(2)}, u32[]{:S(2)}) collective-permute-start(bf16[256,256]{1,0:T(8,128)(2,1)S(1)} %get-tuple-element.38.own), channel_id=1, source_target_pairs={{0,1},{1,0},{2,3},{3,2},{4,5},{5,4},{6,7},{7,6},{8,9},{9,8},{10,11... | collective-permute-start | bytes 393224 | tf_op jit(solution)/shard_map/ppermute | solution.py:237
  45.0 2.3 %collective-permute-start.9 = (bf16[256,256]{1,0:T(8,128)(2,1)S(1)}, bf16[256,256]{1,0:T(8,128)(2,1)S(1)}, u32[]{:S(2)}, u32[]{:S(2)}) collective-permute-start(bf16[256,256]{1,0:T(8,128)(2,1)S(1)} %get-tuple-element.38.own), channel_id=1, source_target_pairs={{1,2},{2,1},{3,4},{4,3},{5,6},{6,5},{7,8},{8,7},{9,10},{10,9},{11,... | collective-permute-start | bytes 393224 | tf_op jit(solution)/shard_map/ppermute | solution.py:238
  69.1 7.5 %collective-permute-start.10 = (bf16[256,256]{1,0:T(8,128)(2,1)S(1)}, bf16[256,256]{1,0:T(8,128)(2,1)S(1)}, u32[]{:S(2)}, u32[]{:S(2)}) collective-permute-start(bf16[256,256]{1,0:T(8,128)(2,1)S(1)} %get-tuple-element.46.half), channel_id=1, source_target_pairs={{16,0},{32,16},{48,32},{64,48},{80,64},{96,80},{112,96},{128,112},... | collective-permute-start | bytes 393224 | tf_op jit(solution)/shard_map/ppermute | solution.py:270

commit v3 on v2

--- a/solution.py
+++ b/solution.py
@@ -7,6 +7,7 @@
 
 
 STEP = 0.3
+PARITY_BIT = 30
 VM = pl.BlockSpec(memory_space=pltpu.VMEM)
 SM = pl.BlockSpec(memory_space=pltpu.SMEM)
 F32 = jnp.float32
@@ -47,6 +48,14 @@
     h_ref[...] = p.astype(BF)
 
 
+def slot_of(code, k):
+    return lax.bitwise_and(lax.shift_right_logical(code[0, 0], jnp.int32(2 * k)), jnp.int32(3))
+
+
+def parity(code):
+    return lax.bitwise_and(lax.shift_right_logical(code[0, 0], jnp.int32(PARITY_BIT)), jnp.int32(1))
+
+
 def fill(hs, own, near, far):
     hs[0] = own[...]
     hs[1] = near[...]
@@ -58,7 +67,7 @@
     h = own[...]
     total[...] = dot(onsite[...], h) + dot_t(h, onsite[...])
     for k in range(left.shape[0]):
-        inner[k] = dot(left[k], hs[slot[k]]).astype(BF)
+        inner[k] = dot(left[k], hs[slot_of(slot, k)]).astype(BF)
 
 
 def finish(total, live, p, w_ref, p_ref, h_ref):
@@ -88,23 +97,25 @@
 
 
 def even_body(slot, live, inner, right_hbm, start, p, w_ref, p_ref, h_ref, right, sem):
-    @pl.when(slot[right.shape[0]] == 0)
+    @pl.when(parity(slot) == 0)
     def _():
-        terms = right.shape[0]
-        copies = [pltpu.make_async_copy(right_hbm.at[k], right.at[k], sem.at[k]) for k in range(terms)]
+        half = right.shape[0] // 2
+        copies = [
+            pltpu.make_async_copy(right_hbm.at[:half], right.at[:half], sem.at[0]),
+            pltpu.make_async_copy(right_hbm.at[half:], right.at[half:], sem.at[1]),
+        ]
         for copy in copies:
             copy.start()
         total = start[...]
-        for k in range(terms):
-            copies[k].wait()
+        for k in range(right.shape[0]):
+            if k in (0, half):
+                copies[k // half].wait()
             total = total + dot_t(inner[k], right[k])
         finish(total, live[0, 0], p[...], w_ref, p_ref, h_ref)
 
 
-def odd_body(slot, live, inner, right, start, p, _, __, w_ref, p_ref, h_ref):
-    @pl.when(slot[right.shape[0]] == 1)
-    def _():
-        finish(outer_sum(inner, right, start), live[0, 0], p[...], w_ref, p_ref, h_ref)
+def odd_body(live, inner, right, start, p, _, __, w_ref, p_ref, h_ref):
+    finish(outer_sum(inner, right, start), live[0, 0], p[...], w_ref, p_ref, h_ref)
 
 
 def product(slot, left, right, own, near, far, onsite, hs):
@@ -112,7 +123,7 @@
     h = own[...]
     total = dot(onsite[...], h) + dot_t(h, onsite[...])
     for k in range(left.shape[0]):
-        part = dot(left[k], hs[slot[k]]).astype(BF)
+        part = dot(left[k], hs[slot_of(slot, k)]).astype(BF)
         total = total + dot_t(part, right[k])
     return total
 
@@ -121,7 +132,7 @@
     sets, (w_ref, p_ref, h_ref, old_w, old_p, hs) = (refs[:6], refs[6:12]), refs[12:]
     for turn, (right, own, near, far, p, w) in enumerate(sets):
 
-        @pl.when(slot[left.shape[0]] == turn)
+        @pl.when(parity(slot) == turn)
         def _():
             total = product(slot, left, right, own, near, far, onsite, hs)
             finish(total, live[0, 0], p[...], w_ref, p_ref, h_ref)
@@ -145,7 +156,7 @@
 def last_body(slot, live, left, right_even, right_odd, own, near, far, onsite, p, p0, w0, w1, g, p_ref, g_ref, hs):
     for turn, right in enumerate((right_even, right_odd)):
 
-        @pl.when(slot[left.shape[0]] == turn)
+        @pl.when(parity(slot) == turn)
         def _():
             total = product(slot, left, right, own, near, far, onsite, hs)
             w = jnp.where(inside(live[0, 0], total.shape), total, 0.0)
@@ -153,7 +164,7 @@
             g_ref[...] = put(g[...], 6, ((p0[...], w), (w0[...], w), (w1[...], w), (w, w)))
 
 
-def coef_body(parts, p0, p1, p2, p3, half_ref, coef_ref):
+def coefficients(parts, p0, p1, p2, p3, half_ref, coef_ref):
     sums = jnp.sum(parts[...], axis=0, keepdims=True)
     v = [sums[:, i : i + 1] for i in range(10)]
     weight, p0w = v[0], [v[1], v[2], v[6]]
@@ -162,7 +173,7 @@
     p2w = [p1w[j] - STEP * ww[1][j] for j in range(3)]
     pw = [p0w, p1w, p2w]
     one = jnp.ones_like(weight)
-    coef, scale = [one], one
+    coef, scale, inverse = [one], one, 1.0 / weight
     energy = one
     for n in range(3):
         c = jnp.zeros_like(one)
@@ -172,8 +183,8 @@
                 t = coef[i] * coef[j]
                 c = c + t * pw[i][j]
                 a = a + t * ww[i][j]
-        energy = c * scale / weight
-        excess = jnp.maximum(a * scale / weight - energy * energy, 0.0)
+        energy = c * scale * inverse
+        excess = jnp.maximum(a * scale * inverse - energy * energy, 0.0)
         scale = scale / (1.0 + STEP * STEP * excess)
         g = STEP * energy
         coef = [g * coef[0]] + [coef[i - 1] + g * coef[i] for i in range(1, n + 1)] + [one]
@@ -188,6 +199,25 @@
     coef_ref[...] = out
 
 
+def coef_even_body(slot, *refs):
+    @pl.when(parity(slot) == 0)
+    def _():
+        coefficients(*refs)
+
+
+def coef_odd_body(slot, half_even, coef_even, parts, p0, p1, p2, p3, half_ref, coef_ref):
+    odd = parity(slot) == 1
+
+    @pl.when(odd)
+    def _():
+        coefficients(parts, p0, p1, p2, p3, half_ref, coef_ref)
+
+    @pl.when(jnp.logical_not(odd))
+    def _():
+        half_ref[...] = half_even[...]
+        coef_ref[...] = coef_even[...]
+
+
 def theta_body(coef, p0, p1, p2, p3, theta_ref):
     c = [coef[i : i + 1, 0:1] for i in range(4)]
     theta_ref[...] = c[0] * p0[...] + c[1] * p1[...] + c[2] * p2[...] + c[3] * p3[...]
@@ -199,12 +229,21 @@
     own_ref[...] = dot_t(jnp.where(cols < rank[0, 0], h, jnp.zeros_like(h)), h)
 
 
-def density_body(rank, beside, own, out_ref):
-    b = beside[...]
+def density_body(slot, rank, beside, beside_odd, own, out_hbm, out, sem):
+    b = jnp.where(parity(slot) == 1, beside_odd[...], beside[...])
     rows = lax.broadcasted_iota(jnp.int32, b.shape, 0)
     kept = jnp.where(rows < rank[0, 0], b, jnp.zeros_like(b))
-    other = lax.dot_general(kept, b, (((0,), (0,)), ((), ())), preferred_element_type=F32)
-    out_ref[...] = own[...] + other
+    half = b.shape[0] // 2
+    copies = []
+    for i in range(2):
+        part = pl.ds(i * half, half)
+        columns = kept[:, i * half : (i + 1) * half]
+        other = lax.dot_general(columns, b, (((0,), (0,)), ((), ())), preferred_element_type=F32)
+        out[part] = own[part] + other
+        copies.append(pltpu.make_async_copy(out.at[part], out_hbm.at[part], sem.at[i]))
+        copies[i].start()
+    for copy in copies:
+        copy.wait()
 
 
 def section_step(left_env, right_out, onsite, start_state, live, rank, shift):
@@ -219,7 +258,9 @@
     far_pairs = [(i, (i - 1 ^ 1) + 1) for i in range(1, blocks) if (i - 1 ^ 1) + 1 < blocks]
     near_shift = 1 - 2 * (blk % 2)
     slot = jnp.where(shift == 0, 0, jnp.where(shift == near_shift, 1, 2)).astype(jnp.int32)
-    slot = jnp.concatenate([slot, jnp.full((1,), sec % 2, jnp.int32)])
+    assert 2 * terms <= PARITY_BIT
+    code = jnp.sum(slot << (2 * jnp.arange(terms, dtype=jnp.int32))) + ((sec % 2) << PARITY_BIT)
+    slot = code.astype(jnp.int32).reshape(1, 1)
     built = right_out.reshape(terms, *square)
     right_odd = lax.ppermute(built, "sec", ahead[1::2])
     state = start_state.reshape(square)
@@ -253,11 +294,11 @@
     args = (slot, live, inner, right_even, total, p0)
     specs = [SM, SM, VM, hbm, VM, VM]
     outs = triple + [((terms, *square), BF)]
-    w0, p1, h1, right_even = call(even_body, outs, args, specs, [pltpu.SemaphoreType.DMA((terms,))])
+    w0, p1, h1, right_even = call(even_body, outs, args, specs, [pltpu.SemaphoreType.DMA((2,))])
     near, far = halo(h1, every[0::2])
     sets = [right_even, h1, near, far, p1, w0]
-    args = (slot, live, inner, right_odd, total, p0, near, far)
-    w0, p1, h1 = call(odd_body, triple, args, [SM, SM] + [VM] * 4 + [hbm] * 2)
+    args = (live, inner, right_odd, total, p0, near, far)
+    w0, p1, h1 = call(odd_body, triple, args, [SM] + [VM] * 4 + [hbm] * 2)
     sets += [right_odd, h1, *halo(h1, every[1::2]), p1, w0]
     outs = triple + [(square, F32)] * 2
     w1, p2, h2, w0, p1 = call(both_body, outs, (slot, live, left, onsite, *sets), [SM, SM] + [VM] * 14, slots)
@@ -266,11 +307,17 @@
     args = (slot, live, left, right_even, right_odd, h2, *halo(h2, every), onsite, p2, p0, w0, w1, gram)
     p3, gram = call(last_body, [(square, F32), (table, F32)], args, [SM, SM] + [VM] * 12, slots)
     parts = lax.all_to_all(gram, "blk", 0, 0, tiled=True)
-    half, coef = call(coef_body, [(square, BF), ((8, 128), F32)], (parts, p0, p1, p2, p3), [VM] * 5)
-    beside = lax.ppermute(half, "sec", ahead)
+    outs = [(square, BF), ((8, 128), F32)]
+    args = (parts, p0, p1, p2, p3)
+    half, coef = call(coef_even_body, outs, (slot, *args), [SM] + [VM] * 5)
+    beside_odd = lax.ppermute(half, "sec", ahead[1::2])
+    half, coef = call(coef_odd_body, outs, (slot, half, coef, *args), [SM] + [VM] * 7)
+    beside = lax.ppermute(half, "sec", ahead[0::2])
     (theta,) = call(theta_body, [(square, F32)], (coef, p0, p1, p2, p3), [VM] * 5)
     (own,) = call(own_body, [(square, F32)], (rank, half), [SM, VM])
-    (density,) = call(density_body, [(square, F32)], (rank, beside, own), [SM, VM, VM])
+    scratch = [pltpu.VMEM(square, F32), pltpu.SemaphoreType.DMA((2,))]
+    args = (slot, rank, beside, beside_odd, own)
+    (density,) = call(density_body, [(square, F32)], args, [SM, SM] + [VM] * 3, scratch, out_specs=[hbm])
     return theta[None, None], coef[4, :1], density[None, None]
 
 

time: 78 us -> 77.7 us (level)
  the two profiles are of different devices: /device:TPU:97 before, /device:TPU:225 now
where the time goes in v3:
time: 77.7 us; the launch traced here: 77.2 us
  starting transfers between devices  23 us (30%)
  waiting for transfers between devices  19.6 us (25%)
  blocking collectives  19 us (24%)
  Pallas kernels  7.67 us (10%)
  local copies, waits for them, and re-layouts  3.86 us (5%)
  between operations  2.81 us (4%)
  other arithmetic  1.3 us (2%)
    all_to_all x1, blocking collectives, section_step(): parts = lax.all_to_all(gram, 'blk', 0, 0, tiled=True)  19 us
    ppermute x4, starting transfers between devices, halo(): near = lax.ppermute(h, axes, pairs(near_pairs))  12.6 us
    ppermute x1, waiting for transfers between devices, section_step(): right_odd = lax.ppermute(built, 'sec', ahead[1::2])  12.3 us
    pallas_call x13, Pallas kernels, call(): pl.pallas_call(body, out_shape=[jax.ShapeDtypeStruct(s, d) for s, d in ou...  7.67 us
    ppermute x1, waiting for transfers between devices, section_step(): beside_odd = lax.ppermute(half, 'sec', ahead[1::2])  3.96 us
    ppermute x1, starting transfers between devices, section_step(): right_even = lax.ppermute(built, 'sec', ahead[0::2])  3.85 us
    unnamed x6, local copies, waits for them, and re-layouts  3.34 us
    ppermute x4, waiting for transfers between devices, halo(): near = lax.ppermute(h, axes, pairs(near_pairs))  3.3 us
  transfers between devices with their start and end apart: 12, of which 4 were waited for; matrix products, arithmetic and copies ran while one was open for 2% of the time, Pallas kernels for 3%

profile of v3, /device:TPU:225, one launch (start us, length us, event | category | flops | bytes accessed | tf_op | source)
XLA Modules:
  0.0 77.2 jit_solution(2661923971412460946)
XLA Ops:
  0.6 3.9 %collective-permute-start.2 = (bf16[14,256,256]{2,1,0:T(8,128)(2,1)}, bf16[14,256,256]{2,1,0:T(8,128)(2,1)}, u32[]{:S(2)}, u32[]{:S(2)}) collective-permute-start(bf16[14,256,256]{2,1,0:T(8,128)(2,1)} %bitcast.20), channel_id=1, source_target_pairs={{16,0},{48,32},{80,64},{112,96},{144,128},{176,160},{208,192},{240... | collective-permute-start | bytes 5505032 | tf_op jit(solution)/shard_map/ppermute | solution.py:286
  4.5 1.3 %collective-permute-start.3 = (bf16[14,256,256]{2,1,0:T(8,128)(2,1)}, bf16[14,256,256]{2,1,0:T(8,128)(2,1)S(1)}, u32[]{:S(2)}, u32[]{:S(2)}) collective-permute-start(bf16[14,256,256]{2,1,0:T(8,128)(2,1)} %bitcast.21), channel_id=1, source_target_pairs={{32,16},{64,48},{96,80},{128,112},{160,144},{192,176},{224,208},{2... | collective-permute-start | bytes 5505032 | tf_op jit(solution)/shard_map/ppermute | solution.py:265
  6.4 0.9 %copy-done.2 = f32[1,1,256,256]{3,2,1,0:T(8,128)S(1)} copy-done((f32[1,1,256,256]{3,2,1,0:T(8,128)S(1)}, f32[1,1,256,256]{3,2,1,0:T(8,128)}, u32[]{:S(2)}) %copy-start.2) | copy-done | bytes 262168
  7.4 3.1 %collective-permute-start = (bf16[256,256]{1,0:T(8,128)(2,1)S(1)}, bf16[256,256]{1,0:T(8,128)(2,1)S(1)}, u32[]{:S(2)}, u32[]{:S(2)}) collective-permute-start(bf16[256,256]{1,0:T(8,128)(2,1)S(1)} %get-tuple-element.28.own), channel_id=1, source_target_pairs={{0,1},{1,0},{2,3},{3,2},{4,5},{5,4},{6,7},{7,6},{8,9},{9,8},{10,11... | collective-permute-start | bytes 393224 | tf_op jit(solution)/shard_map/ppermute | solution.py:278
  10.5 0.7 collective-permute-start.1
  11.2 1.3 %fusion.1 = s32[]{:T(128)} fusion(s32[14]{0:T(128)} %param.13, s32[]{:T(128)S(6)} %sub.3), kind=kLoop, calls=%fused_computation.3 | loop fusion | flops 97 | bytes 64 | tf_op jit(solution)/shard_map/reduce_sum | solution.py:262
  13.2 1.5 %copy-done = bf16[1,14,1,256,256]{4,3,2,1,0:T(8,128)(2,1)S(1)} copy-done((bf16[1,14,1,256,256]{4,3,2,1,0:T(8,128)(2,1)S(1)}, bf16[1,14,1,256,256]{4,3,2,1,0:T(8,128)(2,1)}, u32[]{:S(2)}) %copy-start) | copy-done | bytes 1835032
  14.7 0.9 %copy-done.1 = bf16[1,1,256,256]{3,2,1,0:T(8,128)(2,1)S(1)} copy-done((bf16[1,1,256,256]{3,2,1,0:T(8,128)(2,1)S(1)}, bf16[1,1,256,256]{3,2,1,0:T(8,128)(2,1)}, u32[]{:S(2)}) %copy-start.1) | copy-done | bytes 131096
  15.9 0.8 %shard_map.96 = (bf16[14,256,256]{2,1,0:T(8,128)(2,1)S(1)}, f32[256,256]{1,0:T(8,128)S(1)}) custom-call(s32[1,1]{1,0:T(1,128)} %bitcast.slot, bf16[14,256,256]{2,1,0:T(8,128)(2,1)S(1)} %get-tuple-element.27.left, bf16[256,256]{1,0:T(8,128)(2,1)S(1)} %get-tuple-element.28.own, bf16[256,256]{1,0:T(8,128)(2,1)S(1)} %collective-permute-done.near, ...), custom_call_target="tpu_custom_call" | custom-call | flops 100000000 | bytes 2359300 | tf_op jit(solution)/shard_map/pallas_call | solution.py:20
  18.1 12.3 %collective-permute-done.3.right.refs_6_.right_odd = bf16[14,256,256]{2,1,0:T(8,128)(2,1)S(1)} collective-permute-done((bf16[14,256,256]{2,1,0:T(8,128)(2,1)}, bf16[14,256,256]{2,1,0:T(8,128)(2,1)S(1)}, u32[]{:S(2)}, u32[]{:S(2)}) %collective-permute-start.3) | collective-permute-done | bytes 1835040 | tf_op jit(solution)/shard_map/ppermute | solution.py:265
  30.4 0.7 shard_map.98
  31.1 3.1 %collective-permute-start.6 = (bf16[256,256]{1,0:T(8,128)(2,1)S(1)}, bf16[256,256]{1,0:T(8,128)(2,1)S(1)}, u32[]{:S(2)}, u32[]{:S(2)}) collective-permute-start(bf16[256,256]{1,0:T(8,128)(2,1)S(1)} %get-tuple-element.37.refs_7_), channel_id=1, source_target_pairs={{16,17},{17,16},{18,19},{19,18},{20,21},{21,20},{22,23},{23,22},{2... | collective-permute-start | bytes 393224 | tf_op jit(solution)/shard_map/ppermute | solution.py:278
  34.9 1.9 %collective-permute-done.6.refs_8_ = bf16[256,256]{1,0:T(8,128)(2,1)S(1)} collective-permute-done((bf16[256,256]{1,0:T(8,128)(2,1)S(1)}, bf16[256,256]{1,0:T(8,128)(2,1)S(1)}, u32[]{:S(2)}, u32[]{:S(2)}) %collective-permute-start.6) | collective-permute-done | bytes 131104 | tf_op jit(solution)/shard_map/ppermute | solution.py:278
  36.8 1.4 %shard_map.99 = (f32[256,256]{1,0:T(8,128)S(1)}, f32[256,256]{1,0:T(8,128)S(1)}, bf16[256,256]{1,0:T(8,128)(2,1)S(1)}, f32[256,256]{1,0:T(8,128)S(1)}, f32[256,256]{1,0:T(8,128)S(1)}) custom-call(s32[1,1]{1,0:T(1,128)} %bitcast.slot, s32[1,1]{1,0:T(1,128)S(6)} %copy.11.live, bf16[14,256,256]{2,1,0:T(8,128)(2,1)S(1)} %get-tuple-element.27.left, ...), custom_call_target="tpu_custom_call" | custom-call | flops 100000000 | bytes 7471112 | tf_op jit(solution)/shard_map/pallas_call | solution.py:20
  38.2 5.7 %collective-permute-start.8 = (bf16[256,256]{1,0:T(8,128)(2,1)S(1)}, bf16[256,256]{1,0:T(8,128)(2,1)S(1)}, u32[]{:S(2)}, u32[]{:S(2)}) collective-permute-start(bf16[256,256]{1,0:T(8,128)(2,1)S(1)} %get-tuple-element.40.own), channel_id=1, source_target_pairs={{0,1},{1,0},{2,3},{3,2},{4,5},{5,4},{6,7},{7,6},{8,9},{9,8},{10,11... | collective-permute-start | bytes 393224 | tf_op jit(solution)/shard_map/ppermute | solution.py:278
  44.9 1.4 %collective-permute-done.8.near = bf16[256,256]{1,0:T(8,128)(2,1)S(1)} collective-permute-done((bf16[256,256]{1,0:T(8,128)(2,1)S(1)}, bf16[256,256]{1,0:T(8,128)(2,1)S(1)}, u32[]{:S(2)}, u32[]{:S(2)}) %collective-permute-start.8) | collective-permute-done | bytes 131104 | tf_op jit(solution)/shard_map/ppermute | solution.py:278
  46.3 1.5 %shard_map.101 = (f32[256,256]{1,0:T(8,128)S(1)}, f32[16,128]{1,0:T(8,128)S(1)}) custom-call(s32[1,1]{1,0:T(1,128)} %bitcast.slot, s32[1,1]{1,0:T(1,128)S(6)} %copy.11.live, bf16[14,256,256]{2,1,0:T(8,128)(2,1)S(1)} %get-tuple-element.27.left, bf16[14,256,256]{2,1,0:T(8,128)(2,1)S(1)} %get-tuple-element.33.refs_0_.right_even, ...), custom_call_target="tpu_custom_call" | custom-call | flops 100000000 | bytes 7086088 | tf_op jit(solution)/shard_map/pallas_call | solution.py:20
  47.8 19.0 %all_to_all.11 = f32[16,1,128]{2,1,0:T(1,128)S(1)} all-to-all(f32[16,1,128]{2,1,0:T(1,128)S(1)} %bitcast.16), channel_id=1, replica_groups=mesh['sec'=32,'blk'=16] {'blk'}, dimensions={0} | all-to-all | bytes 16384 | tf_op jit(solution)/shard_map/all_to_all | solution.py:309
  66.8 0.7 shard_map.103
  67.5 1.3 %collective-permute-start.10 = (bf16[256,256]{1,0:T(8,128)(2,1)S(1)}, bf16[256,256]{1,0:T(8,128)(2,1)S(1)}, u32[]{:S(2)}, u32[]{:S(2)}) collective-permute-start(bf16[256,256]{1,0:T(8,128)(2,1)S(1)} %get-tuple-element.50.half), channel_id=1, source_target_pairs={{16,0},{48,32},{80,64},{112,96},{144,128},{176,160},{208,192},{240... | collective-permute-start | bytes 393224 | tf_op jit(solution)/shard_map/ppermute | solution.py:315
  68.8 1.3 %collective-permute-start.11 = (bf16[256,256]{1,0:T(8,128)(2,1)S(1)}, bf16[256,256]{1,0:T(8,128)(2,1)S(1)}, u32[]{:S(2)}, u32[]{:S(2)}) collective-permute-start(bf16[256,256]{1,0:T(8,128)(2,1)S(1)} %get-tuple-element.47.half_even), channel_id=1, source_target_pairs={{32,16},{64,48},{96,80},{128,112},{160,144},{192,176},{224,208},{2... | collective-permute-start | bytes 393224 | tf_op jit(solution)/shard_map/ppermute | solution.py:313
  71.3 0.8 %shard_map.104 = f32[256,256]{1,0:T(8,128)} custom-call(f32[8,128]{1,0:T(8,128)S(1)} %get-tuple-element.49.coef, f32[256,256]{1,0:T(8,128)S(1)} %get-tuple-element.32.p.p0.refs_1_, f32[256,256]{1,0:T(8,128)S(1)} %get-tuple-element.45.refs_2_.p1, f32[256,256]{1,0:T(8,128)S(1)} %get-tuple-element.41.p.refs_3_.p2, f32[256,256]{1,0:T(8,128)S(1)} %get-tuple-element.46.refs_4_.p3), custom_call_target="tpu_custom_call" | custom-call | flops 100000000 | bytes 1052672 | tf_op jit(solution)/shard_map/pallas_call | solution.py:20
  72.3 4.0 %collective-permute-done.11.beside_odd = bf16[256,256]{1,0:T(8,128)(2,1)S(1)} collective-permute-done((bf16[256,256]{1,0:T(8,128)(2,1)S(1)}, bf16[256,256]{1,0:T(8,128)(2,1)S(1)}, u32[]{:S(2)}, u32[]{:S(2)}) %collective-permute-start.11) | collective-permute-done | bytes 131104 | tf_op jit(solution)/shard_map/ppermute | solution.py:313
  76.3 0.9 %shard_map.106 = f32[256,256]{1,0:T(8,128)} custom-call(s32[1,1]{1,0:T(1,128)} %bitcast.slot, s32[1,1]{1,0:T(1,128)S(6)} %copy.12.rank, bf16[256,256]{1,0:T(8,128)(2,1)S(1)} %collective-permute-done.10.beside, bf16[256,256]{1,0:T(8,128)(2,1)S(1)} %collective-permute-done.11.beside_odd, f32[256,256]{1,0:T(8,128)S(1)} %shard_map.105.own), custom_call_target="tpu_custom_call" | custom-call | flops 100000000 | bytes 524296 | tf_op jit(solution)/shard_map/pallas_call | solution.py:20
  (22 shorter events, 4.1 us)
Async XLA Ops:
  0.6 16.1 %collective-permute-start.2 = (bf16[14,256,256]{2,1,0:T(8,128)(2,1)}, bf16[14,256,256]{2,1,0:T(8,128)(2,1)}, u32[]{:S(2)}, u32[]{:S(2)}) collective-permute-start(bf16[14,256,256]{2,1,0:T(8,128)(2,1)} %bitcast.20), channel_id=1, source_target_pairs={{16,0},{48,32},{80,64},{112,96},{144,128},{176,160},{208,192},{240... | collective-permute-start | bytes 5505032 | tf_op jit(solution)/shard_map/ppermute | solution.py:286
  4.5 26.0 %collective-permute-start.3 = (bf16[14,256,256]{2,1,0:T(8,128)(2,1)}, bf16[14,256,256]{2,1,0:T(8,128)(2,1)S(1)}, u32[]{:S(2)}, u32[]{:S(2)}) collective-permute-start(bf16[14,256,256]{2,1,0:T(8,128)(2,1)} %bitcast.21), channel_id=1, source_target_pairs={{32,16},{64,48},{96,80},{128,112},{160,144},{192,176},{224,208},{2... | collective-permute-start | bytes 5505032 | tf_op jit(solution)/shard_map/ppermute | solution.py:265
  6.4 1.0 %copy-start.2 = (f32[1,1,256,256]{3,2,1,0:T(8,128)S(1)}, f32[1,1,256,256]{3,2,1,0:T(8,128)}, u32[]{:S(2)}) copy-start(f32[1,1,256,256]{3,2,1,0:T(8,128)} %param.10) | copy-start | bytes 786436
  7.4 8.5 %collective-permute-start = (bf16[256,256]{1,0:T(8,128)(2,1)S(1)}, bf16[256,256]{1,0:T(8,128)(2,1)S(1)}, u32[]{:S(2)}, u32[]{:S(2)}) collective-permute-start(bf16[256,256]{1,0:T(8,128)(2,1)S(1)} %get-tuple-element.28.own), channel_id=1, source_target_pairs={{0,1},{1,0},{2,3},{3,2},{4,5},{5,4},{6,7},{7,6},{8,9},{9,8},{10,11... | collective-permute-start | bytes 393224 | tf_op jit(solution)/shard_map/ppermute | solution.py:278
  10.5 5.4 %collective-permute-start.1 = (bf16[256,256]{1,0:T(8,128)(2,1)S(1)}, bf16[256,256]{1,0:T(8,128)(2,1)S(1)}, u32[]{:S(2)}, u32[]{:S(2)}) collective-permute-start(bf16[256,256]{1,0:T(8,128)(2,1)S(1)} %get-tuple-element.28.own), channel_id=1, source_target_pairs={{1,2},{2,1},{3,4},{4,3},{5,6},{6,5},{7,8},{8,7},{9,10},{10,9},{11,... | collective-permute-start | bytes 393224 | tf_op jit(solution)/shard_map/ppermute | solution.py:279
  13.2 1.5 %copy-start = (bf16[1,14,1,256,256]{4,3,2,1,0:T(8,128)(2,1)S(1)}, bf16[1,14,1,256,256]{4,3,2,1,0:T(8,128)(2,1)}, u32[]{:S(2)}) copy-start(bf16[1,14,1,256,256]{4,3,2,1,0:T(8,128)(2,1)} %param.7) | copy-start | bytes 5505028
  14.7 0.9 %copy-start.1 = (bf16[1,1,256,256]{3,2,1,0:T(8,128)(2,1)S(1)}, bf16[1,1,256,256]{3,2,1,0:T(8,128)(2,1)}, u32[]{:S(2)}) copy-start(bf16[1,1,256,256]{3,2,1,0:T(8,128)(2,1)} %param.9) | copy-start | bytes 393220
  16.8 13.7 %collective-permute-start.4 = (bf16[256,256]{1,0:T(8,128)(2,1)S(1)}, bf16[256,256]{1,0:T(8,128)(2,1)S(1)}, u32[]{:S(2)}, u32[]{:S(2)}) collective-permute-start(bf16[256,256]{1,0:T(8,128)(2,1)S(1)} %get-tuple-element.34.refs_1_), channel_id=1, source_target_pairs={{0,1},{1,0},{2,3},{3,2},{4,5},{5,4},{6,7},{7,6},{8,9},{9,8},{10,11... | collective-permute-start | bytes 393224 | tf_op jit(solution)/shard_map/ppermute | solution.py:278
  17.4 13.0 %collective-permute-start.5 = (bf16[256,256]{1,0:T(8,128)(2,1)S(1)}, bf16[256,256]{1,0:T(8,128)(2,1)S(1)}, u32[]{:S(2)}, u32[]{:S(2)}) collective-permute-start(bf16[256,256]{1,0:T(8,128)(2,1)S(1)} %get-tuple-element.34.refs_1_), channel_id=1, source_target_pairs={{1,2},{2,1},{3,4},{4,3},{5,6},{6,5},{7,8},{8,7},{9,10},{10,9},{11,... | collective-permute-start | bytes 393224 | tf_op jit(solution)/shard_map/ppermute | solution.py:279
  31.1 5.7 %collective-permute-start.6 = (bf16[256,256]{1,0:T(8,128)(2,1)S(1)}, bf16[256,256]{1,0:T(8,128)(2,1)S(1)}, u32[]{:S(2)}, u32[]{:S(2)}) collective-permute-start(bf16[256,256]{1,0:T(8,128)(2,1)S(1)} %get-tuple-element.37.refs_7_), channel_id=1, source_target_pairs={{16,17},{17,16},{18,19},{19,18},{20,21},{21,20},{22,23},{23,22},{2... | collective-permute-start | bytes 393224 | tf_op jit(solution)/shard_map/ppermute | solution.py:278
  34.3 2.6 %collective-permute-start.7 = (bf16[256,256]{1,0:T(8,128)(2,1)S(1)}, bf16[256,256]{1,0:T(8,128)(2,1)S(1)}, u32[]{:S(2)}, u32[]{:S(2)}) collective-permute-start(bf16[256,256]{1,0:T(8,128)(2,1)S(1)} %get-tuple-element.37.refs_7_), channel_id=1, source_target_pairs={{17,18},{18,17},{19,20},{20,19},{21,22},{22,21},{23,24},{24,23},{2... | collective-permute-start | bytes 393224 | tf_op jit(solution)/shard_map/ppermute | solution.py:279
  38.2 8.1 %collective-permute-start.8 = (bf16[256,256]{1,0:T(8,128)(2,1)S(1)}, bf16[256,256]{1,0:T(8,128)(2,1)S(1)}, u32[]{:S(2)}, u32[]{:S(2)}) collective-permute-start(bf16[256,256]{1,0:T(8,128)(2,1)S(1)} %get-tuple-element.40.own), channel_id=1, source_target_pairs={{0,1},{1,0},{2,3},{3,2},{4,5},{5,4},{6,7},{7,6},{8,9},{9,8},{10,11... | collective-permute-start | bytes 393224 | tf_op jit(solution)/shard_map/ppermute | solution.py:278
  43.9 2.3 %collective-permute-start.9 = (bf16[256,256]{1,0:T(8,128)(2,1)S(1)}, bf16[256,256]{1,0:T(8,128)(2,1)S(1)}, u32[]{:S(2)}, u32[]{:S(2)}) collective-permute-start(bf16[256,256]{1,0:T(8,128)(2,1)S(1)} %get-tuple-element.40.own), channel_id=1, source_target_pairs={{1,2},{2,1},{3,4},{4,3},{5,6},{6,5},{7,8},{8,7},{9,10},{10,9},{11,... | collective-permute-start | bytes 393224 | tf_op jit(solution)/shard_map/ppermute | solution.py:279
  67.5 4.8 %collective-permute-start.10 = (bf16[256,256]{1,0:T(8,128)(2,1)S(1)}, bf16[256,256]{1,0:T(8,128)(2,1)S(1)}, u32[]{:S(2)}, u32[]{:S(2)}) collective-permute-start(bf16[256,256]{1,0:T(8,128)(2,1)S(1)} %get-tuple-element.50.half), channel_id=1, source_target_pairs={{16,0},{48,32},{80,64},{112,96},{144,128},{176,160},{208,192},{240... | collective-permute-start | bytes 393224 | tf_op jit(solution)/shard_map/ppermute | solution.py:315
  68.8 7.5 %collective-permute-start.11 = (bf16[256,256]{1,0:T(8,128)(2,1)S(1)}, bf16[256,256]{1,0:T(8,128)(2,1)S(1)}, u32[]{:S(2)}, u32[]{:S(2)}) collective-permute-start(bf16[256,256]{1,0:T(8,128)(2,1)S(1)} %get-tuple-element.47.half_even), channel_id=1, source_target_pairs={{32,16},{64,48},{96,80},{128,112},{160,144},{192,176},{224,208},{2... | collective-permute-start | bytes 393224 | tf_op jit(solution)/shard_map/ppermute | solution.py:313

commit v4 on v3

--- a/solution.py
+++ b/solution.py
@@ -114,8 +114,10 @@
         finish(total, live[0, 0], p[...], w_ref, p_ref, h_ref)
 
 
-def odd_body(live, inner, right, start, p, _, __, w_ref, p_ref, h_ref):
-    finish(outer_sum(inner, right, start), live[0, 0], p[...], w_ref, p_ref, h_ref)
+def odd_body(slot, live, inner, right, start, p, _, __, w_ref, p_ref, h_ref):
+    @pl.when(parity(slot) == 1)
+    def _():
+        finish(outer_sum(inner, right, start), live[0, 0], p[...], w_ref, p_ref, h_ref)
 
 
 def product(slot, left, right, own, near, far, onsite, hs):
@@ -147,7 +149,7 @@
     return out
 
 
-def gram_body(p0, w0, w1, g_ref):
+def gram_body(_, p0, w0, w1, g_ref):
     a, b, c = p0[...], w0[...], w1[...]
     pairs = ((a, a), (a, b), (a, c), (b, b), (b, c), (c, c))
     g_ref[...] = put(jnp.zeros(g_ref.shape, F32), 0, pairs)
@@ -218,9 +220,10 @@
         coef_ref[...] = coef_even[...]
 
 
-def theta_body(coef, p0, p1, p2, p3, theta_ref):
+def theta_body(coef, p0, p1, p2, p3, theta_ref, energy_ref):
     c = [coef[i : i + 1, 0:1] for i in range(4)]
     theta_ref[...] = c[0] * p0[...] + c[1] * p1[...] + c[2] * p2[...] + c[3] * p3[...]
+    energy_ref[...] = coef[4:5, 0:1]
 
 
 def own_body(rank, half, own_ref):
@@ -297,13 +300,13 @@
     w0, p1, h1, right_even = call(even_body, outs, args, specs, [pltpu.SemaphoreType.DMA((2,))])
     near, far = halo(h1, every[0::2])
     sets = [right_even, h1, near, far, p1, w0]
-    args = (live, inner, right_odd, total, p0, near, far)
-    w0, p1, h1 = call(odd_body, triple, args, [SM] + [VM] * 4 + [hbm] * 2)
+    args = (slot, live, inner, right_odd, total, p0, near, far)
+    w0, p1, h1 = call(odd_body, triple, args, [SM, SM] + [VM] * 4 + [hbm] * 2)
     sets += [right_odd, h1, *halo(h1, every[1::2]), p1, w0]
     outs = triple + [(square, F32)] * 2
     w1, p2, h2, w0, p1 = call(both_body, outs, (slot, live, left, onsite, *sets), [SM, SM] + [VM] * 14, slots)
     table = (blocks, 128)
-    (gram,) = call(gram_body, [(table, F32)], (p0, w0, w1), [VM] * 3)
+    (gram,) = call(gram_body, [(table, F32)], (rank, p0, w0, w1), [SM] + [VM] * 3)
     args = (slot, live, left, right_even, right_odd, h2, *halo(h2, every), onsite, p2, p0, w0, w1, gram)
     p3, gram = call(last_body, [(square, F32), (table, F32)], args, [SM, SM] + [VM] * 12, slots)
     parts = lax.all_to_all(gram, "blk", 0, 0, tiled=True)
@@ -313,12 +316,13 @@
     beside_odd = lax.ppermute(half, "sec", ahead[1::2])
     half, coef = call(coef_odd_body, outs, (slot, half, coef, *args), [SM] + [VM] * 7)
     beside = lax.ppermute(half, "sec", ahead[0::2])
-    (theta,) = call(theta_body, [(square, F32)], (coef, p0, p1, p2, p3), [VM] * 5)
+    outs = [(square, F32), ((1, 1), F32)]
+    theta, energy = call(theta_body, outs, (coef, p0, p1, p2, p3), [VM] * 5)
     (own,) = call(own_body, [(square, F32)], (rank, half), [SM, VM])
     scratch = [pltpu.VMEM(square, F32), pltpu.SemaphoreType.DMA((2,))]
     args = (slot, rank, beside, beside_odd, own)
     (density,) = call(density_body, [(square, F32)], args, [SM, SM] + [VM] * 3, scratch, out_specs=[hbm])
-    return theta[None, None], coef[4, :1], density[None, None]
+    return theta[None, None], energy.reshape(1), density[None, None]
 
 
 def solution(mesh):

time: 77.7 us -> 77.8 us (level)
  the two profiles are of different devices: /device:TPU:225 before, /device:TPU:353 now
where the time goes in v4:
time: 77.8 us; the launch traced here: 77.2 us
  starting transfers between devices  23 us (30%)
  waiting for transfers between devices  20.1 us (26%)
  blocking collectives  19 us (24%)
  Pallas kernels  7.7 us (10%)
  local copies, waits for them, and re-layouts  3.34 us (4%)
  between operations  2.8 us (4%)
  other arithmetic  1.3 us (2%)
    all_to_all x1, blocking collectives, section_step(): parts = lax.all_to_all(gram, 'blk', 0, 0, tiled=True)  19 us
    ppermute x4, starting transfers between devices, halo(): near = lax.ppermute(h, axes, pairs(near_pairs))  12.6 us
    ppermute x1, waiting for transfers between devices, section_step(): right_odd = lax.ppermute(built, 'sec', ahead[1::2])  12.3 us
    pallas_call x13, Pallas kernels, call(): pl.pallas_call(body, out_shape=[jax.ShapeDtypeStruct(s, d) for s, d in ou...  7.7 us
    ppermute x1, waiting for transfers between devices, section_step(): beside_odd = lax.ppermute(half, 'sec', ahead[1::2])  5.12 us
    ppermute x1, starting transfers between devices, section_step(): right_even = lax.ppermute(built, 'sec', ahead[0::2])  3.86 us
    unnamed x6, local copies, waits for them, and re-layouts  3.34 us
    ppermute x4, starting transfers between devices, halo(): far = lax.ppermute(h, axes, pairs(far_pairs))  2.68 us
  transfers between devices with their start and end apart: 12, of which 4 were waited for; matrix products, arithmetic and copies ran while one was open for 2% of the time, Pallas kernels for 3%

profile of v4, /device:TPU:353, one launch (start us, length us, event | category | flops | bytes accessed | tf_op | source)
XLA Modules:
  0.0 77.2 jit_solution(7636636539537215765)
XLA Ops:
  0.6 3.9 %collective-permute-start.2 = (bf16[14,256,256]{2,1,0:T(8,128)(2,1)}, bf16[14,256,256]{2,1,0:T(8,128)(2,1)}, u32[]{:S(2)}, u32[]{:S(2)}) collective-permute-start(bf16[14,256,256]{2,1,0:T(8,128)(2,1)} %bitcast.19), channel_id=1, source_target_pairs={{16,0},{48,32},{80,64},{112,96},{144,128},{176,160},{208,192},{240... | collective-permute-start | bytes 5505032 | tf_op jit(solution)/shard_map/ppermute | solution.py:289
  4.5 1.3 %collective-permute-start.3 = (bf16[14,256,256]{2,1,0:T(8,128)(2,1)}, bf16[14,256,256]{2,1,0:T(8,128)(2,1)S(1)}, u32[]{:S(2)}, u32[]{:S(2)}) collective-permute-start(bf16[14,256,256]{2,1,0:T(8,128)(2,1)} %bitcast.20), channel_id=1, source_target_pairs={{32,16},{64,48},{96,80},{128,112},{160,144},{192,176},{224,208},{2... | collective-permute-start | bytes 5505032 | tf_op jit(solution)/shard_map/ppermute | solution.py:268
  6.4 0.9 %copy-done.2 = f32[1,1,256,256]{3,2,1,0:T(8,128)S(1)} copy-done((f32[1,1,256,256]{3,2,1,0:T(8,128)S(1)}, f32[1,1,256,256]{3,2,1,0:T(8,128)}, u32[]{:S(2)}) %copy-start.2) | copy-done | bytes 262168
  7.4 3.1 %collective-permute-start = (bf16[256,256]{1,0:T(8,128)(2,1)S(1)}, bf16[256,256]{1,0:T(8,128)(2,1)S(1)}, u32[]{:S(2)}, u32[]{:S(2)}) collective-permute-start(bf16[256,256]{1,0:T(8,128)(2,1)S(1)} %get-tuple-element.30.own), channel_id=1, source_target_pairs={{0,1},{1,0},{2,3},{3,2},{4,5},{5,4},{6,7},{7,6},{8,9},{9,8},{10,11... | collective-permute-start | bytes 393224 | tf_op jit(solution)/shard_map/ppermute | solution.py:281
  11.2 1.3 %fusion.1 = s32[]{:T(128)} fusion(s32[14]{0:T(128)} %param.13, s32[]{:T(128)S(6)} %sub.3), kind=kLoop, calls=%fused_computation.3 | loop fusion | flops 97 | bytes 64 | tf_op jit(solution)/shard_map/reduce_sum | solution.py:265
  13.2 1.5 %copy-done = bf16[1,14,1,256,256]{4,3,2,1,0:T(8,128)(2,1)S(1)} copy-done((bf16[1,14,1,256,256]{4,3,2,1,0:T(8,128)(2,1)S(1)}, bf16[1,14,1,256,256]{4,3,2,1,0:T(8,128)(2,1)}, u32[]{:S(2)}) %copy-start) | copy-done | bytes 1835032
  14.7 0.9 %copy-done.1 = bf16[1,1,256,256]{3,2,1,0:T(8,128)(2,1)S(1)} copy-done((bf16[1,1,256,256]{3,2,1,0:T(8,128)(2,1)S(1)}, bf16[1,1,256,256]{3,2,1,0:T(8,128)(2,1)}, u32[]{:S(2)}) %copy-start.1) | copy-done | bytes 131096
  15.9 0.8 %shard_map.96 = (bf16[14,256,256]{2,1,0:T(8,128)(2,1)S(1)}, f32[256,256]{1,0:T(8,128)S(1)}) custom-call(s32[1,1]{1,0:T(1,128)} %bitcast.slot, bf16[14,256,256]{2,1,0:T(8,128)(2,1)S(1)} %get-tuple-element.29.left, bf16[256,256]{1,0:T(8,128)(2,1)S(1)} %get-tuple-element.30.own, bf16[256,256]{1,0:T(8,128)(2,1)S(1)} %collective-permute-done.near, ...), custom_call_target="tpu_custom_call" | custom-call | flops 100000000 | bytes 2359300 | tf_op jit(solution)/shard_map/pallas_call | solution.py:20
  16.8 0.7 collective-permute-start.4
  18.1 12.3 %collective-permute-done.3.right.refs_6_.right_odd = bf16[14,256,256]{2,1,0:T(8,128)(2,1)S(1)} collective-permute-done((bf16[14,256,256]{2,1,0:T(8,128)(2,1)}, bf16[14,256,256]{2,1,0:T(8,128)(2,1)S(1)}, u32[]{:S(2)}, u32[]{:S(2)}) %collective-permute-start.3) | collective-permute-done | bytes 1835040 | tf_op jit(solution)/shard_map/ppermute | solution.py:268
  30.5 0.7 shard_map.98
  31.1 3.1 %collective-permute-start.6 = (bf16[256,256]{1,0:T(8,128)(2,1)S(1)}, bf16[256,256]{1,0:T(8,128)(2,1)S(1)}, u32[]{:S(2)}, u32[]{:S(2)}) collective-permute-start(bf16[256,256]{1,0:T(8,128)(2,1)S(1)} %get-tuple-element.39.refs_7_), channel_id=1, source_target_pairs={{16,17},{17,16},{18,19},{19,18},{20,21},{21,20},{22,23},{23,22},{2... | collective-permute-start | bytes 393224 | tf_op jit(solution)/shard_map/ppermute | solution.py:281
  34.9 1.9 %collective-permute-done.6.refs_8_ = bf16[256,256]{1,0:T(8,128)(2,1)S(1)} collective-permute-done((bf16[256,256]{1,0:T(8,128)(2,1)S(1)}, bf16[256,256]{1,0:T(8,128)(2,1)S(1)}, u32[]{:S(2)}, u32[]{:S(2)}) %collective-permute-start.6) | collective-permute-done | bytes 131104 | tf_op jit(solution)/shard_map/ppermute | solution.py:281
  36.9 1.4 %shard_map.99 = (f32[256,256]{1,0:T(8,128)S(1)}, f32[256,256]{1,0:T(8,128)S(1)}, bf16[256,256]{1,0:T(8,128)(2,1)S(1)}, f32[256,256]{1,0:T(8,128)S(1)}, f32[256,256]{1,0:T(8,128)S(1)}) custom-call(s32[1,1]{1,0:T(1,128)} %bitcast.slot, s32[1,1]{1,0:T(1,128)S(6)} %copy.11.live, bf16[14,256,256]{2,1,0:T(8,128)(2,1)S(1)} %get-tuple-element.29.left, ...), custom_call_target="tpu_custom_call" | custom-call | flops 100000000 | bytes 7471112 | tf_op jit(solution)/shard_map/pallas_call | solution.py:20
  38.2 5.7 %collective-permute-start.8 = (bf16[256,256]{1,0:T(8,128)(2,1)S(1)}, bf16[256,256]{1,0:T(8,128)(2,1)S(1)}, u32[]{:S(2)}, u32[]{:S(2)}) collective-permute-start(bf16[256,256]{1,0:T(8,128)(2,1)S(1)} %get-tuple-element.42.own), channel_id=1, source_target_pairs={{0,1},{1,0},{2,3},{3,2},{4,5},{5,4},{6,7},{7,6},{8,9},{9,8},{10,11... | collective-permute-start | bytes 393224 | tf_op jit(solution)/shard_map/ppermute | solution.py:281
  45.6 0.7 collective-permute-done.8.near
  46.3 1.5 %shard_map.101 = (f32[256,256]{1,0:T(8,128)S(1)}, f32[16,128]{1,0:T(8,128)S(1)}) custom-call(s32[1,1]{1,0:T(1,128)} %bitcast.slot, s32[1,1]{1,0:T(1,128)S(6)} %copy.11.live, bf16[14,256,256]{2,1,0:T(8,128)(2,1)S(1)} %get-tuple-element.29.left, bf16[14,256,256]{2,1,0:T(8,128)(2,1)S(1)} %get-tuple-element.35.refs_0_.right_even, ...), custom_call_target="tpu_custom_call" | custom-call | flops 100000000 | bytes 7086088 | tf_op jit(solution)/shard_map/pallas_call | solution.py:20
  47.8 19.0 %all_to_all.11 = f32[16,1,128]{2,1,0:T(1,128)S(1)} all-to-all(f32[16,1,128]{2,1,0:T(1,128)S(1)} %bitcast.16), channel_id=1, replica_groups=mesh['sec'=32,'blk'=16] {'blk'}, dimensions={0} | all-to-all | bytes 16384 | tf_op jit(solution)/shard_map/all_to_all | solution.py:312
  66.8 0.7 shard_map.103
  67.5 1.3 %collective-permute-start.10 = (bf16[256,256]{1,0:T(8,128)(2,1)S(1)}, bf16[256,256]{1,0:T(8,128)(2,1)S(1)}, u32[]{:S(2)}, u32[]{:S(2)}) collective-permute-start(bf16[256,256]{1,0:T(8,128)(2,1)S(1)} %get-tuple-element.54.half), channel_id=1, source_target_pairs={{16,0},{48,32},{80,64},{112,96},{144,128},{176,160},{208,192},{240... | collective-permute-start | bytes 393224 | tf_op jit(solution)/shard_map/ppermute | solution.py:318
  68.8 1.3 %collective-permute-start.11 = (bf16[256,256]{1,0:T(8,128)(2,1)S(1)}, bf16[256,256]{1,0:T(8,128)(2,1)S(1)}, u32[]{:S(2)}, u32[]{:S(2)}) collective-permute-start(bf16[256,256]{1,0:T(8,128)(2,1)S(1)} %get-tuple-element.49.half_even), channel_id=1, source_target_pairs={{32,16},{64,48},{96,80},{128,112},{160,144},{192,176},{224,208},{2... | collective-permute-start | bytes 393224 | tf_op jit(solution)/shard_map/ppermute | solution.py:316
  70.3 0.9 %shard_map.104 = (f32[256,256]{1,0:T(8,128)}, f32[1,1]{1,0:T(1,128)}) custom-call(f32[8,128]{1,0:T(8,128)S(1)} %get-tuple-element.51.coef, f32[256,256]{1,0:T(8,128)S(1)} %get-tuple-element.34.p.p0.refs_1_, f32[256,256]{1,0:T(8,128)S(1)} %get-tuple-element.47.refs_2_.p1, f32[256,256]{1,0:T(8,128)S(1)} %get-tuple-element.43.p.refs_3_.p2, ...), custom_call_target="tpu_custom_call" | custom-call | flops 100000000 | bytes 1052672 | tf_op jit(solution)/shard_map/pallas_call | solution.py:20
  71.2 5.1 %collective-permute-done.11.beside_odd = bf16[256,256]{1,0:T(8,128)(2,1)S(1)} collective-permute-done((bf16[256,256]{1,0:T(8,128)(2,1)S(1)}, bf16[256,256]{1,0:T(8,128)(2,1)S(1)}, u32[]{:S(2)}, u32[]{:S(2)}) %collective-permute-start.11) | collective-permute-done | bytes 131104 | tf_op jit(solution)/shard_map/ppermute | solution.py:316
  76.3 0.9 %shard_map.106 = f32[256,256]{1,0:T(8,128)} custom-call(s32[1,1]{1,0:T(1,128)} %bitcast.slot, s32[1,1]{1,0:T(1,128)S(6)} %copy.12._.rank, bf16[256,256]{1,0:T(8,128)(2,1)S(1)} %collective-permute-done.10.beside, bf16[256,256]{1,0:T(8,128)(2,1)S(1)} %collective-permute-done.11.beside_odd, f32[256,256]{1,0:T(8,128)S(1)} %shard_map.105.own), custom_call_target="tpu_custom_call" | custom-call | flops 100000000 | bytes 524296 | tf_op jit(solution)/shard_map/pallas_call | solution.py:20
  (21 shorter events, 3.6 us)
Async XLA Ops:
  0.6 16.1 %collective-permute-start.2 = (bf16[14,256,256]{2,1,0:T(8,128)(2,1)}, bf16[14,256,256]{2,1,0:T(8,128)(2,1)}, u32[]{:S(2)}, u32[]{:S(2)}) collective-permute-start(bf16[14,256,256]{2,1,0:T(8,128)(2,1)} %bitcast.19), channel_id=1, source_target_pairs={{16,0},{48,32},{80,64},{112,96},{144,128},{176,160},{208,192},{240... | collective-permute-start | bytes 5505032 | tf_op jit(solution)/shard_map/ppermute | solution.py:289
  4.5 26.0 %collective-permute-start.3 = (bf16[14,256,256]{2,1,0:T(8,128)(2,1)}, bf16[14,256,256]{2,1,0:T(8,128)(2,1)S(1)}, u32[]{:S(2)}, u32[]{:S(2)}) collective-permute-start(bf16[14,256,256]{2,1,0:T(8,128)(2,1)} %bitcast.20), channel_id=1, source_target_pairs={{32,16},{64,48},{96,80},{128,112},{160,144},{192,176},{224,208},{2... | collective-permute-start | bytes 5505032 | tf_op jit(solution)/shard_map/ppermute | solution.py:268
  6.4 1.0 %copy-start.2 = (f32[1,1,256,256]{3,2,1,0:T(8,128)S(1)}, f32[1,1,256,256]{3,2,1,0:T(8,128)}, u32[]{:S(2)}) copy-start(f32[1,1,256,256]{3,2,1,0:T(8,128)} %param.10) | copy-start | bytes 786436
  7.4 8.5 %collective-permute-start = (bf16[256,256]{1,0:T(8,128)(2,1)S(1)}, bf16[256,256]{1,0:T(8,128)(2,1)S(1)}, u32[]{:S(2)}, u32[]{:S(2)}) collective-permute-start(bf16[256,256]{1,0:T(8,128)(2,1)S(1)} %get-tuple-element.30.own), channel_id=1, source_target_pairs={{0,1},{1,0},{2,3},{3,2},{4,5},{5,4},{6,7},{7,6},{8,9},{9,8},{10,11... | collective-permute-start | bytes 393224 | tf_op jit(solution)/shard_map/ppermute | solution.py:281
  10.5 5.4 %collective-permute-start.1 = (bf16[256,256]{1,0:T(8,128)(2,1)S(1)}, bf16[256,256]{1,0:T(8,128)(2,1)S(1)}, u32[]{:S(2)}, u32[]{:S(2)}) collective-permute-start(bf16[256,256]{1,0:T(8,128)(2,1)S(1)} %get-tuple-element.30.own), channel_id=1, source_target_pairs={{1,2},{2,1},{3,4},{4,3},{5,6},{6,5},{7,8},{8,7},{9,10},{10,9},{11,... | collective-permute-start | bytes 393224 | tf_op jit(solution)/shard_map/ppermute | solution.py:282
  13.2 1.5 %copy-start = (bf16[1,14,1,256,256]{4,3,2,1,0:T(8,128)(2,1)S(1)}, bf16[1,14,1,256,256]{4,3,2,1,0:T(8,128)(2,1)}, u32[]{:S(2)}) copy-start(bf16[1,14,1,256,256]{4,3,2,1,0:T(8,128)(2,1)} %param.7) | copy-start | bytes 5505028
  14.7 0.9 %copy-start.1 = (bf16[1,1,256,256]{3,2,1,0:T(8,128)(2,1)S(1)}, bf16[1,1,256,256]{3,2,1,0:T(8,128)(2,1)}, u32[]{:S(2)}) copy-start(bf16[1,1,256,256]{3,2,1,0:T(8,128)(2,1)} %param.9) | copy-start | bytes 393220
  16.8 13.7 %collective-permute-start.4 = (bf16[256,256]{1,0:T(8,128)(2,1)S(1)}, bf16[256,256]{1,0:T(8,128)(2,1)S(1)}, u32[]{:S(2)}, u32[]{:S(2)}) collective-permute-start(bf16[256,256]{1,0:T(8,128)(2,1)S(1)} %get-tuple-element.36.refs_1_), channel_id=1, source_target_pairs={{0,1},{1,0},{2,3},{3,2},{4,5},{5,4},{6,7},{7,6},{8,9},{9,8},{10,11... | collective-permute-start | bytes 393224 | tf_op jit(solution)/shard_map/ppermute | solution.py:281
  17.4 13.0 %collective-permute-start.5 = (bf16[256,256]{1,0:T(8,128)(2,1)S(1)}, bf16[256,256]{1,0:T(8,128)(2,1)S(1)}, u32[]{:S(2)}, u32[]{:S(2)}) collective-permute-start(bf16[256,256]{1,0:T(8,128)(2,1)S(1)} %get-tuple-element.36.refs_1_), channel_id=1, source_target_pairs={{1,2},{2,1},{3,4},{4,3},{5,6},{6,5},{7,8},{8,7},{9,10},{10,9},{11,... | collective-permute-start | bytes 393224 | tf_op jit(solution)/shard_map/ppermute | solution.py:282
  31.1 5.7 %collective-permute-start.6 = (bf16[256,256]{1,0:T(8,128)(2,1)S(1)}, bf16[256,256]{1,0:T(8,128)(2,1)S(1)}, u32[]{:S(2)}, u32[]{:S(2)}) collective-permute-start(bf16[256,256]{1,0:T(8,128)(2,1)S(1)} %get-tuple-element.39.refs_7_), channel_id=1, source_target_pairs={{16,17},{17,16},{18,19},{19,18},{20,21},{21,20},{22,23},{23,22},{2... | collective-permute-start | bytes 393224 | tf_op jit(solution)/shard_map/ppermute | solution.py:281
  34.3 2.6 %collective-permute-start.7 = (bf16[256,256]{1,0:T(8,128)(2,1)S(1)}, bf16[256,256]{1,0:T(8,128)(2,1)S(1)}, u32[]{:S(2)}, u32[]{:S(2)}) collective-permute-start(bf16[256,256]{1,0:T(8,128)(2,1)S(1)} %get-tuple-element.39.refs_7_), channel_id=1, source_target_pairs={{17,18},{18,17},{19,20},{20,19},{21,22},{22,21},{23,24},{24,23},{2... | collective-permute-start | bytes 393224 | tf_op jit(solution)/shard_map/ppermute | solution.py:282
  38.2 8.1 %collective-permute-start.8 = (bf16[256,256]{1,0:T(8,128)(2,1)S(1)}, bf16[256,256]{1,0:T(8,128)(2,1)S(1)}, u32[]{:S(2)}, u32[]{:S(2)}) collective-permute-start(bf16[256,256]{1,0:T(8,128)(2,1)S(1)} %get-tuple-element.42.own), channel_id=1, source_target_pairs={{0,1},{1,0},{2,3},{3,2},{4,5},{5,4},{6,7},{7,6},{8,9},{9,8},{10,11... | collective-permute-start | bytes 393224 | tf_op jit(solution)/shard_map/ppermute | solution.py:281
  43.9 2.3 %collective-permute-start.9 = (bf16[256,256]{1,0:T(8,128)(2,1)S(1)}, bf16[256,256]{1,0:T(8,128)(2,1)S(1)}, u32[]{:S(2)}, u32[]{:S(2)}) collective-permute-start(bf16[256,256]{1,0:T(8,128)(2,1)S(1)} %get-tuple-element.42.own), channel_id=1, source_target_pairs={{1,2},{2,1},{3,4},{4,3},{5,6},{6,5},{7,8},{8,7},{9,10},{10,9},{11,... | collective-permute-start | bytes 393224 | tf_op jit(solution)/shard_map/ppermute | solution.py:282
  67.5 3.7 %collective-permute-start.10 = (bf16[256,256]{1,0:T(8,128)(2,1)S(1)}, bf16[256,256]{1,0:T(8,128)(2,1)S(1)}, u32[]{:S(2)}, u32[]{:S(2)}) collective-permute-start(bf16[256,256]{1,0:T(8,128)(2,1)S(1)} %get-tuple-element.54.half), channel_id=1, source_target_pairs={{16,0},{48,32},{80,64},{112,96},{144,128},{176,160},{208,192},{240... | collective-permute-start | bytes 393224 | tf_op jit(solution)/shard_map/ppermute | solution.py:318
  68.8 7.5 %collective-permute-start.11 = (bf16[256,256]{1,0:T(8,128)(2,1)S(1)}, bf16[256,256]{1,0:T(8,128)(2,1)S(1)}, u32[]{:S(2)}, u32[]{:S(2)}) collective-permute-start(bf16[256,256]{1,0:T(8,128)(2,1)S(1)} %get-tuple-element.49.half_even), channel_id=1, source_target_pairs={{32,16},{64,48},{96,80},{128,112},{160,144},{192,176},{224,208},{2... | collective-permute-start | bytes 393224 | tf_op jit(solution)/shard_map/ppermute | solution.py:316
